TPU v7x, 32 devices: a whole 2x2x4 slice. The times are simulated.
32 devices in a mesh: gy: 4 (over y, core), gx: 8 (over z, x).
Axes of the slice: x: 2, y: 2, z: 4, core: 2. Of those that a mesh axis runs over, the one named last changes fastest.
Arguments:
- phase: float32 [2, 128, 1024], P(None, 'gy', 'gx'), may hold values from -1.5 to 1.5
- velocity: float32 [2, 128, 1024], P(None, 'gy', 'gx'), may hold values from -2 to 2
- offsets: int32 [2, 4], replicated, may hold values from 0 to 1020, as said below
Outputs:
- phase_out: float32 [2, 128, 1024], P(None, 'gy', 'gx')
Inputs may be any that keep to these rules, and one draw needn't show every extreme that they name: `offsets`: every offset is a multiple of 2 ** 2.
All inputs are finite; a program needn't handle non-finite values.
Results may differ from a plain program's by a relative error of at most 0.00014.
Values sent between devices are 32-bit elements; how exact they have to be, the bound alone decides.
No kernel may reach another device: no remote copies, remote signals or barrier semaphores. Data moves between devices by JAX's collectives and lax.ppermute only.
A program may use at most 64 MiB of HBM per device.

v0:
```python
import jax
import jax.numpy as jnp
from jax import lax
from jax.sharding import PartitionSpec as P

STEPS = 2
ITERS = 2
LEVELS = 3
COARSE = 4


RELAXATION = 0.8
DIFFUSION = 4.0
VERTICAL = 1.0
REACTION = 0.5
ADVECTION = 0.5


def padded(cells, sides, width):
    for axis, dim in sides:
        count = lax.axis_size(axis)
        head = lax.slice_in_dim(cells, 0, width, axis=dim)
        tail = lax.slice_in_dim(cells, cells.shape[dim] - width, cells.shape[dim], axis=dim)
        cells = jnp.concatenate(
            [
                lax.ppermute(tail, axis, [(i, (i + 1) % count) for i in range(count)]),
                cells,
                lax.ppermute(head, axis, [((i + 1) % count, i) for i in range(count)]),
            ],
            axis=dim,
        )
    return cells


def sheared(bottom_row, upper_row, offsets_now, anchor, columns):
    breadth = bottom_row.shape[1]
    device_row = lax.axis_index("gy")
    row_count = lax.axis_size("gy")
    below_shift = offsets_now[device_row]
    above_shift = offsets_now[(device_row + 1) % row_count]
    local_columns = jnp.arange(columns, dtype=jnp.int32)
    down_index = (anchor + below_shift + local_columns) % breadth
    up_index = (anchor - above_shift + local_columns) % breadth
    down_window = jnp.take(bottom_row, down_index, axis=1)
    up_window = jnp.take(upper_row, up_index, axis=1)
    stacked = jnp.stack([down_window, up_window], axis=1)
    rims = padded(stacked, (("gy", 1),), 1)
    return (rims[:, 0, :], rims[:, 3, :])


def stencil(field, below_row, above_row, across, coupling):
    diagonal = 1.0 + 4.0 * coupling + 2.0 * VERTICAL
    column_pad = jnp.concatenate([below_row[:, None, :], field, above_row[:, None, :]], axis=1)
    beside = column_pad[:, 2:, :] + column_pad[:, :-2, :] + across
    vertical_sum = jnp.roll(field, 1, 0) + jnp.roll(field, -1, 0)
    return diagonal * field - coupling * beside - VERTICAL * vertical_sum


def operate(field, offsets_now, coupling):
    columns = field.shape[2]
    margins = padded(field, (("gx", 2),), 1)
    bottom_full, upper_full = (
        lax.all_gather(field[:, 0, :], "gx", axis=1, tiled=True),
        lax.all_gather(field[:, -1, :], "gx", axis=1, tiled=True),
    )
    right_field = margins[:, :, 2:]
    left_field = margins[:, :, :-2]
    below_row, above_row = sheared(
        bottom_full, upper_full, offsets_now, lax.axis_index("gx") * columns, columns
    )
    across = right_field + left_field
    return (stencil(field, below_row, above_row, across, coupling), right_field, left_field)


def operate_strip(field, offsets_now, coupling):
    below_row, above_row = sheared(field[:, 0, :], field[:, -1, :], offsets_now, 0, field.shape[2])
    across = jnp.roll(field, 1, 2) + jnp.roll(field, -1, 2)
    return stencil(field, below_row, above_row, across, coupling)


def coarsest(residual, offsets_now, coupling):
    diagonal = 1.0 + 4.0 * coupling + 2.0 * VERTICAL
    columns = residual.shape[2]
    gathered = lax.all_gather(residual, "gx", axis=2, tiled=True)
    estimate = RELAXATION * gathered / diagonal
    for sweep_index in range(COARSE - 1):
        estimate = (
            estimate
            + RELAXATION * (gathered - operate_strip(estimate, offsets_now, coupling)) / diagonal
        )
    return lax.dynamic_slice_in_dim(estimate, lax.axis_index("gx") * columns, columns, 2)


def vcycle(residual, offsets_raw, layer_index):
    factor = 2**layer_index
    coupling = DIFFUSION / 4.0**layer_index
    diagonal = 1.0 + 4.0 * coupling + 2.0 * VERTICAL
    offsets_now = offsets_raw // factor
    if layer_index == LEVELS - 1:
        return coarsest(residual, offsets_now, coupling)
    estimate = RELAXATION * residual / diagonal
    defect = residual - operate(estimate, offsets_now, coupling)[0]
    planes, height, breadth = defect.shape
    coarser = defect.reshape(planes, height // 2, 2, breadth // 2, 2).mean(axis=(2, 4))
    correction = vcycle(coarser, offsets_raw, layer_index + 1)
    estimate = estimate + jnp.repeat(jnp.repeat(correction, 2, axis=1), 2, axis=2)
    estimate = (
        estimate + RELAXATION * (residual - operate(estimate, offsets_now, coupling)[0]) / diagonal
    )
    return estimate


def total_inner(first_field, second_field):
    return lax.psum(jnp.sum(first_field * second_field), ("gy", "gx"))


def local(phase, velocity, offsets):
    phase_now = phase
    for time_step in range(STEPS):
        offsets_raw = offsets[time_step]
        applied, right_field, left_field = operate(phase_now, offsets_raw, DIFFUSION)
        source = (
            phase_now
            + REACTION * (phase_now - phase_now * phase_now * phase_now)
            - ADVECTION * velocity * (right_field - left_field)
        )
        residual = source - applied
        precond = vcycle(residual, offsets_raw, 0)
        projected = total_inner(residual, precond)
        direction = precond
        for iteration in range(ITERS):
            image = operate(direction, offsets_raw, DIFFUSION)[0]
            step_size = projected / total_inner(direction, image)
            phase_now = phase_now + step_size * direction
            residual = residual - step_size * image
            if iteration + 1 < ITERS:
                precond = vcycle(residual, offsets_raw, 0)
                following = total_inner(residual, precond)
                direction = precond + following / projected * direction
                projected = following
    return phase_now


def solution(mesh):
    placed = (P(None, "gy", "gx"), P(None, "gy", "gx"), P())
    return jax.shard_map(
        local, mesh=mesh, in_specs=placed, out_specs=P(None, "gy", "gx"), check_vma=False
    )
```

profile of v0, /device:TPU:0, one launch (start us, length us, event | category | flops | bytes accessed | tf_op | source)
XLA Modules:
  0.0 1669.3 jit_solution(4805464784161272798)
XLA Ops:
  10.4 31.3 %all-gather.1 = f32[2,1,1024]{0,2,1:T(8,128)S(1)} all-gather(f32[2,1,128]{0,2,1:T(8,128)S(1)} %copy.2969), channel_id=3, replica_groups=mesh['gy'=4,'gx'=8] {'gx'}, dimensions={2}, use_global_device_ids=true | all-gather | bytes 9216 | tf_op jit(solution)/shard_map/all_gather | solution.py:64
  42.5 31.5 %all-gather = f32[2,1,1024]{0,2,1:T(8,128)S(1)} all-gather(f32[2,1,128]{0,2,1:T(8,128)S(1)} %copy.2968), channel_id=2, replica_groups=mesh['gy'=4,'gx'=8] {'gx'}, dimensions={2}, use_global_device_ids=true | all-gather | bytes 9216 | tf_op jit(solution)/shard_map/all_gather | solution.py:63
  87.8 20.9 %all-gather.2 = f32[2,1,1024]{2,1,0:T(1,128)S(1)} all-gather(f32[2,1,128]{2,1,0:T(1,128)S(1)} %get-tuple-element.104), channel_id=4, replica_groups=mesh['gy'=4,'gx'=8] {'gx'}, dimensions={2}, use_global_device_ids=true | all-gather | bytes 9216 | tf_op jit(solution)/shard_map/all_gather | solution.py:63
  139.5 30.8 %all-gather.5 = f32[2,1,512]{0,1,2:T(1,128)S(1)} all-gather(f32[2,1,64]{0,1,2:T(1,128)S(1)} %copy.2705), channel_id=7, replica_groups=mesh['gy'=4,'gx'=8] {'gx'}, dimensions={2}, use_global_device_ids=true | all-gather | bytes 4608 | tf_op jit(solution)/shard_map/all_gather | solution.py:64
  171.0 30.7 %all-gather.4 = f32[2,1,512]{0,1,2:T(1,128)S(1)} all-gather(f32[2,1,64]{0,1,2:T(1,128)S(1)} %copy.2702), channel_id=6, replica_groups=mesh['gy'=4,'gx'=8] {'gx'}, dimensions={2}, use_global_device_ids=true | all-gather | bytes 4608 | tf_op jit(solution)/shard_map/all_gather | solution.py:63
  204.7 30.7 %all_gather.150 = f32[2,8,256]{1,0,2:T(2,128)S(1)} all-gather(f32[2,8,32]{1,0,2:T(2,128)S(1)} %copy.2708), channel_id=1, replica_groups=mesh['gy'=4,'gx'=8] {'gx'}, dimensions={2}, use_global_device_ids=true | all-gather | bytes 18432 | tf_op jit(solution)/shard_map/all_gather | solution.py:84
  256.7 30.7 %all-gather.7 = f32[2,1,512]{0,1,2:T(1,128)S(1)} all-gather(f32[2,1,64]{0,1,2:T(1,128)S(1)} %copy.2731), channel_id=9, replica_groups=mesh['gy'=4,'gx'=8] {'gx'}, dimensions={2}, use_global_device_ids=true | all-gather | bytes 4608 | tf_op jit(solution)/shard_map/all_gather | solution.py:64
  288.2 30.8 %all-gather.6 = f32[2,1,512]{0,1,2:T(1,128)S(1)} all-gather(f32[2,1,64]{0,1,2:T(1,128)S(1)} %copy.2728), channel_id=8, replica_groups=mesh['gy'=4,'gx'=8] {'gx'}, dimensions={2}, use_global_device_ids=true | all-gather | bytes 4608 | tf_op jit(solution)/shard_map/all_gather | solution.py:63
  321.5 20.9 %all-gather.8 = f32[2,1,1024]{2,1,0:T(1,128)S(1)} all-gather(f32[2,1,128]{2,1,0:T(1,128)S(1)} %get-tuple-element.98), channel_id=10, replica_groups=mesh['gy'=4,'gx'=8] {'gx'}, dimensions={2}, use_global_device_ids=true | all-gather | bytes 9216 | tf_op jit(solution)/shard_map/all_gather | solution.py:63
  342.4 16.3 all-gather.9
  367.5 19.4 %all-gather.10 = f32[2,1,1024]{2,1,0:T(1,128)S(1)} all-gather(f32[2,1,128]{2,1,0:T(1,128)S(1)} %get-tuple-element.90), channel_id=12, replica_groups=mesh['gy'=4,'gx'=8] {'gx'}, dimensions={2}, use_global_device_ids=true | all-gather | bytes 9216 | tf_op jit(solution)/shard_map/all_gather | solution.py:63
  386.9 16.3 all-gather.11
  412.5 38.7 %all-reduce.1 = (f32[]{:T(128)}, f32[]{:T(128)}) all-reduce(f32[]{:T(128)} %get-tuple-element.11, f32[]{:T(128)} %get-tuple-element.10), channel_id=1, replica_groups=mesh['gy'=4,'gx'=8] {'gy','gx'}, use_global_device_ids=true, to_apply=%region_3.7 | all-reduce | flops 2 | bytes 16 | tf_op jit(solution)/shard_map/psum | solution.py:114
  452.7 19.5 %all-gather.12 = f32[2,1,1024]{2,1,0:T(1,128)S(1)} all-gather(f32[2,1,128]{2,1,0:T(1,128)S(1)} %get-tuple-element.86), channel_id=14, replica_groups=mesh['gy'=4,'gx'=8] {'gx'}, dimensions={2}, use_global_device_ids=true | all-gather | bytes 9216 | tf_op jit(solution)/shard_map/all_gather | solution.py:63
  472.3 16.3 all-gather.13
  503.1 30.8 %all-gather.15 = f32[2,1,512]{0,1,2:T(1,128)S(1)} all-gather(f32[2,1,64]{0,1,2:T(1,128)S(1)} %copy.2751), channel_id=17, replica_groups=mesh['gy'=4,'gx'=8] {'gx'}, dimensions={2}, use_global_device_ids=true | all-gather | bytes 4608 | tf_op jit(solution)/shard_map/all_gather | solution.py:64
  534.7 30.7 %all-gather.14 = f32[2,1,512]{0,1,2:T(1,128)S(1)} all-gather(f32[2,1,64]{0,1,2:T(1,128)S(1)} %copy.2748), channel_id=16, replica_groups=mesh['gy'=4,'gx'=8] {'gx'}, dimensions={2}, use_global_device_ids=true | all-gather | bytes 4608 | tf_op jit(solution)/shard_map/all_gather | solution.py:63
  568.4 30.7 %all_gather.161 = f32[2,8,256]{1,0,2:T(2,128)S(1)} all-gather(f32[2,8,32]{1,0,2:T(2,128)S(1)} %copy.2754), channel_id=1, replica_groups=mesh['gy'=4,'gx'=8] {'gx'}, dimensions={2}, use_global_device_ids=true | all-gather | bytes 18432 | tf_op jit(solution)/shard_map/all_gather | solution.py:84
  620.3 30.7 %all-gather.17 = f32[2,1,512]{0,1,2:T(1,128)S(1)} all-gather(f32[2,1,64]{0,1,2:T(1,128)S(1)} %copy.2777), channel_id=19, replica_groups=mesh['gy'=4,'gx'=8] {'gx'}, dimensions={2}, use_global_device_ids=true | all-gather | bytes 4608 | tf_op jit(solution)/shard_map/all_gather | solution.py:64
  651.8 30.8 %all-gather.16 = f32[2,1,512]{0,1,2:T(1,128)S(1)} all-gather(f32[2,1,64]{0,1,2:T(1,128)S(1)} %copy.2774), channel_id=18, replica_groups=mesh['gy'=4,'gx'=8] {'gx'}, dimensions={2}, use_global_device_ids=true | all-gather | bytes 4608 | tf_op jit(solution)/shard_map/all_gather | solution.py:63
  685.1 20.9 %all-gather.18 = f32[2,1,1024]{2,1,0:T(1,128)S(1)} all-gather(f32[2,1,128]{2,1,0:T(1,128)S(1)} %get-tuple-element.78), channel_id=20, replica_groups=mesh['gy'=4,'gx'=8] {'gx'}, dimensions={2}, use_global_device_ids=true | all-gather | bytes 9216 | tf_op jit(solution)/shard_map/all_gather | solution.py:63
  706.0 16.3 all-gather.19
  731.6 38.6 %psum.58 = f32[]{:T(128)} all-reduce(f32[]{:T(128)} %get-tuple-element.23), channel_id=1, replica_groups=mesh['gy'=4,'gx'=8] {'gy','gx'}, use_global_device_ids=true, to_apply=%region_9.13 | all-reduce | flops 1 | bytes 8 | tf_op jit(solution)/shard_map/psum | solution.py:114
  771.7 19.5 %all-gather.20 = f32[2,1,1024]{2,1,0:T(1,128)S(1)} all-gather(f32[2,1,128]{2,1,0:T(1,128)S(1)} %get-tuple-element.74), channel_id=22, replica_groups=mesh['gy'=4,'gx'=8] {'gx'}, dimensions={2}, use_global_device_ids=true | all-gather | bytes 9216 | tf_op jit(solution)/shard_map/all_gather | solution.py:63
  791.2 16.3 all-gather.21
  816.9 38.3 %psum.59 = f32[]{:T(128)} all-reduce(f32[]{:T(128)} %fusion.65), channel_id=1, replica_groups=mesh['gy'=4,'gx'=8] {'gy','gx'}, use_global_device_ids=true, to_apply=%region_11.15 | all-reduce | flops 1 | bytes 8 | tf_op jit(solution)/shard_map/psum | solution.py:114
  856.6 19.5 %all-gather.22 = f32[2,1,1024]{2,1,0:T(1,128)S(1)} all-gather(f32[2,1,128]{2,1,0:T(1,128)S(1)} %get-tuple-element.68), channel_id=24, replica_groups=mesh['gy'=4,'gx'=8] {'gx'}, dimensions={2}, use_global_device_ids=true | all-gather | bytes 9216 | tf_op jit(solution)/shard_map/all_gather | solution.py:63
  876.1 16.3 all-gather.23
  901.2 19.4 %all-gather.24 = f32[2,1,1024]{2,1,0:T(1,128)S(1)} all-gather(f32[2,1,128]{2,1,0:T(1,128)S(1)} %get-tuple-element.62), channel_id=26, replica_groups=mesh['gy'=4,'gx'=8] {'gx'}, dimensions={2}, use_global_device_ids=true | all-gather | bytes 9216 | tf_op jit(solution)/shard_map/all_gather | solution.py:63
  951.4 30.8 %all-gather.27 = f32[2,1,512]{0,1,2:T(1,128)S(1)} all-gather(f32[2,1,64]{0,1,2:T(1,128)S(1)} %copy.2801), channel_id=29, replica_groups=mesh['gy'=4,'gx'=8] {'gx'}, dimensions={2}, use_global_device_ids=true | all-gather | bytes 4608 | tf_op jit(solution)/shard_map/all_gather | solution.py:64
  983.0 30.7 %all-gather.26 = f32[2,1,512]{0,1,2:T(1,128)S(1)} all-gather(f32[2,1,64]{0,1,2:T(1,128)S(1)} %copy.2798), channel_id=28, replica_groups=mesh['gy'=4,'gx'=8] {'gx'}, dimensions={2}, use_global_device_ids=true | all-gather | bytes 4608 | tf_op jit(solution)/shard_map/all_gather | solution.py:63
  1016.7 30.7 %all_gather.174 = f32[2,8,256]{1,0,2:T(2,128)S(1)} all-gather(f32[2,8,32]{1,0,2:T(2,128)S(1)} %copy.2804), channel_id=1, replica_groups=mesh['gy'=4,'gx'=8] {'gx'}, dimensions={2}, use_global_device_ids=true | all-gather | bytes 18432 | tf_op jit(solution)/shard_map/all_gather | solution.py:84
  1068.6 30.7 %all-gather.29 = f32[2,1,512]{0,1,2:T(1,128)S(1)} all-gather(f32[2,1,64]{0,1,2:T(1,128)S(1)} %copy.2827), channel_id=31, replica_groups=mesh['gy'=4,'gx'=8] {'gx'}, dimensions={2}, use_global_device_ids=true | all-gather | bytes 4608 | tf_op jit(solution)/shard_map/all_gather | solution.py:64
  1100.1 30.8 %all-gather.28 = f32[2,1,512]{0,1,2:T(1,128)S(1)} all-gather(f32[2,1,64]{0,1,2:T(1,128)S(1)} %copy.2824), channel_id=30, replica_groups=mesh['gy'=4,'gx'=8] {'gx'}, dimensions={2}, use_global_device_ids=true | all-gather | bytes 4608 | tf_op jit(solution)/shard_map/all_gather | solution.py:63
  1133.4 20.9 %all-gather.30 = f32[2,1,1024]{2,1,0:T(1,128)S(1)} all-gather(f32[2,1,128]{2,1,0:T(1,128)S(1)} %get-tuple-element.56), channel_id=32, replica_groups=mesh['gy'=4,'gx'=8] {'gx'}, dimensions={2}, use_global_device_ids=true | all-gather | bytes 9216 | tf_op jit(solution)/shard_map/all_gather | solution.py:63
  1179.5 19.4 %all-gather.32 = f32[2,1,1024]{2,1,0:T(1,128)S(1)} all-gather(f32[2,1,128]{2,1,0:T(1,128)S(1)} %get-tuple-element.48), channel_id=34, replica_groups=mesh['gy'=4,'gx'=8] {'gx'}, dimensions={2}, use_global_device_ids=true | all-gather | bytes 9216 | tf_op jit(solution)/shard_map/all_gather | solution.py:63
  1224.4 38.8 %all-reduce = (f32[]{:T(128)}, f32[]{:T(128)}) all-reduce(f32[]{:T(128)} %get-tuple-element.8, f32[]{:T(128)} %get-tuple-element.6), channel_id=1, replica_groups=mesh['gy'=4,'gx'=8] {'gy','gx'}, use_global_device_ids=true, to_apply=%region_15.19 | all-reduce | flops 2 | bytes 16 | tf_op jit(solution)/shard_map/psum | solution.py:114
  1264.7 19.5 %all-gather.34 = f32[2,1,1024]{2,1,0:T(1,128)S(1)} all-gather(f32[2,1,128]{2,1,0:T(1,128)S(1)} %get-tuple-element.44), channel_id=36, replica_groups=mesh['gy'=4,'gx'=8] {'gx'}, dimensions={2}, use_global_device_ids=true | all-gather | bytes 9216 | tf_op jit(solution)/shard_map/all_gather | solution.py:63
  1284.3 16.3 all-gather.35
  1315.1 30.8 %all-gather.37 = f32[2,1,512]{0,1,2:T(1,128)S(1)} all-gather(f32[2,1,64]{0,1,2:T(1,128)S(1)} %copy.2847), channel_id=39, replica_groups=mesh['gy'=4,'gx'=8] {'gx'}, dimensions={2}, use_global_device_ids=true | all-gather | bytes 4608 | tf_op jit(solution)/shard_map/all_gather | solution.py:64
  1346.7 30.7 %all-gather.36 = f32[2,1,512]{0,1,2:T(1,128)S(1)} all-gather(f32[2,1,64]{0,1,2:T(1,128)S(1)} %copy.2844), channel_id=38, replica_groups=mesh['gy'=4,'gx'=8] {'gx'}, dimensions={2}, use_global_device_ids=true | all-gather | bytes 4608 | tf_op jit(solution)/shard_map/all_gather | solution.py:63
  1380.3 30.7 %all_gather.185 = f32[2,8,256]{1,0,2:T(2,128)S(1)} all-gather(f32[2,8,32]{1,0,2:T(2,128)S(1)} %copy.2850), channel_id=1, replica_groups=mesh['gy'=4,'gx'=8] {'gx'}, dimensions={2}, use_global_device_ids=true | all-gather | bytes 18432 | tf_op jit(solution)/shard_map/all_gather | solution.py:84
  1432.3 30.7 %all-gather.39 = f32[2,1,512]{0,1,2:T(1,128)S(1)} all-gather(f32[2,1,64]{0,1,2:T(1,128)S(1)} %copy.2873), channel_id=41, replica_groups=mesh['gy'=4,'gx'=8] {'gx'}, dimensions={2}, use_global_device_ids=true | all-gather | bytes 4608 | tf_op jit(solution)/shard_map/all_gather | solution.py:64
  1463.8 30.9 %all-gather.38 = f32[2,1,512]{0,1,2:T(1,128)S(1)} all-gather(f32[2,1,64]{0,1,2:T(1,128)S(1)} %copy.2870), channel_id=40, replica_groups=mesh['gy'=4,'gx'=8] {'gx'}, dimensions={2}, use_global_device_ids=true | all-gather | bytes 4608 | tf_op jit(solution)/shard_map/all_gather | solution.py:63
  1497.2 21.0 %all-gather.40 = f32[2,1,1024]{2,1,0:T(1,128)S(1)} all-gather(f32[2,1,128]{2,1,0:T(1,128)S(1)} %get-tuple-element.36), channel_id=42, replica_groups=mesh['gy'=4,'gx'=8] {'gx'}, dimensions={2}, use_global_device_ids=true | all-gather | bytes 9216 | tf_op jit(solution)/shard_map/all_gather | solution.py:63
  1543.8 38.2 %psum.62 = f32[]{:T(128)} all-reduce(f32[]{:T(128)} %get-tuple-element.16), channel_id=1, replica_groups=mesh['gy'=4,'gx'=8] {'gy','gx'}, use_global_device_ids=true, to_apply=%region_21.25 | all-reduce | flops 1 | bytes 8 | tf_op jit(solution)/shard_map/psum | solution.py:114
  1583.5 19.5 %all-gather.42 = f32[2,1,1024]{2,1,0:T(1,128)S(1)} all-gather(f32[2,1,128]{2,1,0:T(1,128)S(1)} %get-tuple-element.32), channel_id=44, replica_groups=mesh['gy'=4,'gx'=8] {'gx'}, dimensions={2}, use_global_device_ids=true | all-gather | bytes 9216 | tf_op jit(solution)/shard_map/all_gather | solution.py:63
  1628.6 38.3 %psum.63 = f32[]{:T(128)} all-reduce(f32[]{:T(128)} %fusion.14), channel_id=1, replica_groups=mesh['gy'=4,'gx'=8] {'gy','gx'}, use_global_device_ids=true, to_apply=%region_23.27 | all-reduce | flops 1 | bytes 8 | tf_op jit(solution)/shard_map/psum | solution.py:114
  (801 shorter events, 369.0 us)
Async XLA Ops:
  0.9 85.7 %collective-permute-start = (f32[2,32,1]{2,1,0:T(8,128)S(1)}, f32[2,32,1]{2,1,0:T(8,128)S(1)}, u32[]{:S(2)}, u32[]{:S(2)}) collective-permute-start(f32[2,32,1]{2,1,0:T(8,128)S(1)} %get-tuple-element.108), channel_id=1, source_target_pairs={{1,0},{2,1},{3,2},{4,3},{5,4},{6,5},{7,6},{0,7},{9,8},{10,9},{11,1... | collective-permute-start | bytes 776 | tf_op jit(solution)/shard_map/ppermute | solution.py:28
  6.9 79.7 %collective-permute-start.1 = (f32[2,32,1]{2,1,0:T(8,128)S(1)}, f32[2,32,1]{2,1,0:T(8,128)S(1)}, u32[]{:S(2)}, u32[]{:S(2)}) collective-permute-start(f32[2,32,1]{2,1,0:T(8,128)S(1)} %get-tuple-element.109), channel_id=1, source_target_pairs={{0,1},{1,2},{2,3},{3,4},{4,5},{5,6},{6,7},{7,0},{8,9},{9,10},{10,1... | collective-permute-start | bytes 776 | tf_op jit(solution)/shard_map/ppermute | solution.py:26
  42.4 44.2 %collective-permute-start.3 = (f32[2,1,128]{2,1,0:T(1,128)S(1)}, f32[2,1,128]{2,1,0:T(1,128)S(1)}, u32[]{:S(2)}, u32[]{:S(2)}) collective-permute-start(f32[2,1,128]{2,1,0:T(1,128)S(1)} %bitcast.402), channel_id=1, source_target_pairs={{0,8},{8,16},{16,24},{24,0},{1,9},{9,17},{17,25},{25,1},{2,10},{10... | collective-permute-start | bytes 3080 | tf_op jit(solution)/shard_map/ppermute | solution.py:26
  74.7 11.9 collective-permute-start.2
  124.9 5.7 collective-permute-start.6
  126.9 6.6 collective-permute-start.7
  136.4 66.2 %collective-permute-start.10 = (f32[2,16,1]{2,1,0:T(8,128)S(1)}, f32[2,16,1]{2,1,0:T(8,128)S(1)}, u32[]{:S(2)}, u32[]{:S(2)}) collective-permute-start(f32[2,16,1]{2,1,0:T(8,128)S(1)} %get-tuple-element.256), channel_id=1, source_target_pairs={{1,0},{2,1},{3,2},{4,3},{5,4},{6,5},{7,6},{0,7},{9,8},{10,9},{11,1... | collective-permute-start | bytes 392 | tf_op jit(solution)/shard_map/ppermute | solution.py:28
  139.5 63.1 %collective-permute-start.11 = (f32[2,16,1]{2,1,0:T(8,128)S(1)}, f32[2,16,1]{2,1,0:T(8,128)S(1)}, u32[]{:S(2)}, u32[]{:S(2)}) collective-permute-start(f32[2,16,1]{2,1,0:T(8,128)S(1)} %get-tuple-element.257), channel_id=1, source_target_pairs={{0,1},{1,2},{2,3},{3,4},{4,5},{5,6},{6,7},{7,0},{8,9},{9,10},{10,1... | collective-permute-start | bytes 392 | tf_op jit(solution)/shard_map/ppermute | solution.py:26
  171.0 31.5 %collective-permute-start.9 = (f32[2,1,64]{2,1,0:T(1,128)S(1)}, f32[2,1,64]{2,1,0:T(1,128)S(1)}, u32[]{:S(2)}, u32[]{:S(2)}) collective-permute-start(f32[2,1,64]{2,1,0:T(1,128)S(1)} %copy.2707), channel_id=1, source_target_pairs={{0,8},{8,16},{16,24},{24,0},{1,9},{9,17},{17,25},{25,1},{2,10},{10... | collective-permute-start | bytes 1544 | tf_op jit(solution)/shard_map/ppermute | solution.py:26
  252.0 67.8 %collective-permute-start.20 = (f32[2,16,1]{2,1,0:T(8,128)S(1)}, f32[2,16,1]{2,1,0:T(8,128)S(1)}, u32[]{:S(2)}, u32[]{:S(2)}) collective-permute-start(f32[2,16,1]{2,1,0:T(8,128)S(1)} %get-tuple-element.226), channel_id=1, source_target_pairs={{1,0},{2,1},{3,2},{4,3},{5,4},{6,5},{7,6},{0,7},{9,8},{10,9},{11,1... | collective-permute-start | bytes 392 | tf_op jit(solution)/shard_map/ppermute | solution.py:28
  256.7 63.1 %collective-permute-start.21 = (f32[2,16,1]{2,1,0:T(8,128)S(1)}, f32[2,16,1]{2,1,0:T(8,128)S(1)}, u32[]{:S(2)}, u32[]{:S(2)}) collective-permute-start(f32[2,16,1]{2,1,0:T(8,128)S(1)} %get-tuple-element.227), channel_id=1, source_target_pairs={{0,1},{1,2},{2,3},{3,4},{4,5},{5,6},{6,7},{7,0},{8,9},{9,10},{10,1... | collective-permute-start | bytes 392 | tf_op jit(solution)/shard_map/ppermute | solution.py:26
  288.2 31.6 %collective-permute-start.19 = (f32[2,1,64]{2,1,0:T(1,128)S(1)}, f32[2,1,64]{2,1,0:T(1,128)S(1)}, u32[]{:S(2)}, u32[]{:S(2)}) collective-permute-start(f32[2,1,64]{2,1,0:T(1,128)S(1)} %copy.2733), channel_id=1, source_target_pairs={{0,8},{8,16},{16,24},{24,0},{1,9},{9,17},{17,25},{25,1},{2,10},{10... | collective-permute-start | bytes 1544 | tf_op jit(solution)/shard_map/ppermute | solution.py:26
  358.7 5.7 collective-permute-start.24
  360.7 6.6 collective-permute-start.25
  403.2 5.9 collective-permute-start.28
  405.2 6.6 collective-permute-start.29
  488.6 5.7 collective-permute-start.32
  490.6 6.6 collective-permute-start.33
  500.0 66.2 %collective-permute-start.36 = (f32[2,16,1]{2,1,0:T(8,128)S(1)}, f32[2,16,1]{2,1,0:T(8,128)S(1)}, u32[]{:S(2)}, u32[]{:S(2)}) collective-permute-start(f32[2,16,1]{2,1,0:T(8,128)S(1)} %get-tuple-element.220), channel_id=1, source_target_pairs={{1,0},{2,1},{3,2},{4,3},{5,4},{6,5},{7,6},{0,7},{9,8},{10,9},{11,1... | collective-permute-start | bytes 392 | tf_op jit(solution)/shard_map/ppermute | solution.py:28
  503.1 63.1 %collective-permute-start.37 = (f32[2,16,1]{2,1,0:T(8,128)S(1)}, f32[2,16,1]{2,1,0:T(8,128)S(1)}, u32[]{:S(2)}, u32[]{:S(2)}) collective-permute-start(f32[2,16,1]{2,1,0:T(8,128)S(1)} %get-tuple-element.221), channel_id=1, source_target_pairs={{0,1},{1,2},{2,3},{3,4},{4,5},{5,6},{6,7},{7,0},{8,9},{9,10},{10,1... | collective-permute-start | bytes 392 | tf_op jit(solution)/shard_map/ppermute | solution.py:26
  534.7 31.5 %collective-permute-start.35 = (f32[2,1,64]{2,1,0:T(1,128)S(1)}, f32[2,1,64]{2,1,0:T(1,128)S(1)}, u32[]{:S(2)}, u32[]{:S(2)}) collective-permute-start(f32[2,1,64]{2,1,0:T(1,128)S(1)} %copy.2753), channel_id=1, source_target_pairs={{0,8},{8,16},{16,24},{24,0},{1,9},{9,17},{17,25},{25,1},{2,10},{10... | collective-permute-start | bytes 1544 | tf_op jit(solution)/shard_map/ppermute | solution.py:26
  615.7 67.7 %collective-permute-start.46 = (f32[2,16,1]{2,1,0:T(8,128)S(1)}, f32[2,16,1]{2,1,0:T(8,128)S(1)}, u32[]{:S(2)}, u32[]{:S(2)}) collective-permute-start(f32[2,16,1]{2,1,0:T(8,128)S(1)} %get-tuple-element.190), channel_id=1, source_target_pairs={{1,0},{2,1},{3,2},{4,3},{5,4},{6,5},{7,6},{0,7},{9,8},{10,9},{11,1... | collective-permute-start | bytes 392 | tf_op jit(solution)/shard_map/ppermute | solution.py:28
  620.3 63.1 %collective-permute-start.47 = (f32[2,16,1]{2,1,0:T(8,128)S(1)}, f32[2,16,1]{2,1,0:T(8,128)S(1)}, u32[]{:S(2)}, u32[]{:S(2)}) collective-permute-start(f32[2,16,1]{2,1,0:T(8,128)S(1)} %get-tuple-element.191), channel_id=1, source_target_pairs={{0,1},{1,2},{2,3},{3,4},{4,5},{5,6},{6,7},{7,0},{8,9},{9,10},{10,1... | collective-permute-start | bytes 392 | tf_op jit(solution)/shard_map/ppermute | solution.py:26
  651.8 31.6 %collective-permute-start.45 = (f32[2,1,64]{2,1,0:T(1,128)S(1)}, f32[2,1,64]{2,1,0:T(1,128)S(1)}, u32[]{:S(2)}, u32[]{:S(2)}) collective-permute-start(f32[2,1,64]{2,1,0:T(1,128)S(1)} %copy.2779), channel_id=1, source_target_pairs={{0,8},{8,16},{16,24},{24,0},{1,9},{9,17},{17,25},{25,1},{2,10},{10... | collective-permute-start | bytes 1544 | tf_op jit(solution)/shard_map/ppermute | solution.py:26
  722.3 5.7 collective-permute-start.50
  724.3 6.6 collective-permute-start.51
  807.5 5.7 collective-permute-start.54
  809.5 6.6 collective-permute-start.55
  894.4 6.6 collective-permute-start.57
  938.9 6.6 collective-permute-start.63
  948.3 66.2 %collective-permute-start.66 = (f32[2,16,1]{2,1,0:T(8,128)S(1)}, f32[2,16,1]{2,1,0:T(8,128)S(1)}, u32[]{:S(2)}, u32[]{:S(2)}) collective-permute-start(f32[2,16,1]{2,1,0:T(8,128)S(1)} %get-tuple-element.184), channel_id=1, source_target_pairs={{1,0},{2,1},{3,2},{4,3},{5,4},{6,5},{7,6},{0,7},{9,8},{10,9},{11,1... | collective-permute-start | bytes 392 | tf_op jit(solution)/shard_map/ppermute | solution.py:28
  951.4 63.1 %collective-permute-start.67 = (f32[2,16,1]{2,1,0:T(8,128)S(1)}, f32[2,16,1]{2,1,0:T(8,128)S(1)}, u32[]{:S(2)}, u32[]{:S(2)}) collective-permute-start(f32[2,16,1]{2,1,0:T(8,128)S(1)} %get-tuple-element.185), channel_id=1, source_target_pairs={{0,1},{1,2},{2,3},{3,4},{4,5},{5,6},{6,7},{7,0},{8,9},{9,10},{10,1... | collective-permute-start | bytes 392 | tf_op jit(solution)/shard_map/ppermute | solution.py:26
  983.0 31.5 %collective-permute-start.65 = (f32[2,1,64]{2,1,0:T(1,128)S(1)}, f32[2,1,64]{2,1,0:T(1,128)S(1)}, u32[]{:S(2)}, u32[]{:S(2)}) collective-permute-start(f32[2,1,64]{2,1,0:T(1,128)S(1)} %copy.2803), channel_id=1, source_target_pairs={{0,8},{8,16},{16,24},{24,0},{1,9},{9,17},{17,25},{25,1},{2,10},{10... | collective-permute-start | bytes 1544 | tf_op jit(solution)/shard_map/ppermute | solution.py:26
  1064.0 67.7 %collective-permute-start.76 = (f32[2,16,1]{2,1,0:T(8,128)S(1)}, f32[2,16,1]{2,1,0:T(8,128)S(1)}, u32[]{:S(2)}, u32[]{:S(2)}) collective-permute-start(f32[2,16,1]{2,1,0:T(8,128)S(1)} %get-tuple-element.154), channel_id=1, source_target_pairs={{1,0},{2,1},{3,2},{4,3},{5,4},{6,5},{7,6},{0,7},{9,8},{10,9},{11,1... | collective-permute-start | bytes 392 | tf_op jit(solution)/shard_map/ppermute | solution.py:28
  1068.6 63.1 %collective-permute-start.77 = (f32[2,16,1]{2,1,0:T(8,128)S(1)}, f32[2,16,1]{2,1,0:T(8,128)S(1)}, u32[]{:S(2)}, u32[]{:S(2)}) collective-permute-start(f32[2,16,1]{2,1,0:T(8,128)S(1)} %get-tuple-element.155), channel_id=1, source_target_pairs={{0,1},{1,2},{2,3},{3,4},{4,5},{5,6},{6,7},{7,0},{8,9},{9,10},{10,1... | collective-permute-start | bytes 392 | tf_op jit(solution)/shard_map/ppermute | solution.py:26
  1100.1 31.6 %collective-permute-start.75 = (f32[2,1,64]{2,1,0:T(1,128)S(1)}, f32[2,1,64]{2,1,0:T(1,128)S(1)}, u32[]{:S(2)}, u32[]{:S(2)}) collective-permute-start(f32[2,1,64]{2,1,0:T(1,128)S(1)} %copy.2829), channel_id=1, source_target_pairs={{0,8},{8,16},{16,24},{24,0},{1,9},{9,17},{17,25},{25,1},{2,10},{10... | collective-permute-start | bytes 1544 | tf_op jit(solution)/shard_map/ppermute | solution.py:26
  1172.6 6.6 collective-permute-start.81
  1215.1 5.7 collective-permute-start.84
  1217.1 6.6 collective-permute-start.85
  1302.6 6.6 collective-permute-start.89
  1312.0 66.2 %collective-permute-start.92 = (f32[2,16,1]{2,1,0:T(8,128)S(1)}, f32[2,16,1]{2,1,0:T(8,128)S(1)}, u32[]{:S(2)}, u32[]{:S(2)}) collective-permute-start(f32[2,16,1]{2,1,0:T(8,128)S(1)} %get-tuple-element.148), channel_id=1, source_target_pairs={{1,0},{2,1},{3,2},{4,3},{5,4},{6,5},{7,6},{0,7},{9,8},{10,9},{11,1... | collective-permute-start | bytes 392 | tf_op jit(solution)/shard_map/ppermute | solution.py:28
  1315.1 63.1 %collective-permute-start.93 = (f32[2,16,1]{2,1,0:T(8,128)S(1)}, f32[2,16,1]{2,1,0:T(8,128)S(1)}, u32[]{:S(2)}, u32[]{:S(2)}) collective-permute-start(f32[2,16,1]{2,1,0:T(8,128)S(1)} %get-tuple-element.149), channel_id=1, source_target_pairs={{0,1},{1,2},{2,3},{3,4},{4,5},{5,6},{6,7},{7,0},{8,9},{9,10},{10,1... | collective-permute-start | bytes 392 | tf_op jit(solution)/shard_map/ppermute | solution.py:26
  1346.6 31.5 %collective-permute-start.91 = (f32[2,1,64]{2,1,0:T(1,128)S(1)}, f32[2,1,64]{2,1,0:T(1,128)S(1)}, u32[]{:S(2)}, u32[]{:S(2)}) collective-permute-start(f32[2,1,64]{2,1,0:T(1,128)S(1)} %copy.2849), channel_id=1, source_target_pairs={{0,8},{8,16},{16,24},{24,0},{1,9},{9,17},{17,25},{25,1},{2,10},{10... | collective-permute-start | bytes 1544 | tf_op jit(solution)/shard_map/ppermute | solution.py:26
  1427.6 67.8 %collective-permute-start.102 = (f32[2,16,1]{2,1,0:T(8,128)S(1)}, f32[2,16,1]{2,1,0:T(8,128)S(1)}, u32[]{:S(2)}, u32[]{:S(2)}) collective-permute-start(f32[2,16,1]{2,1,0:T(8,128)S(1)} %get-tuple-element.118), channel_id=1, source_target_pairs={{1,0},{2,1},{3,2},{4,3},{5,4},{6,5},{7,6},{0,7},{9,8},{10,9},{11,1... | collective-permute-start | bytes 392 | tf_op jit(solution)/shard_map/ppermute | solution.py:28
  1432.3 63.1 %collective-permute-start.103 = (f32[2,16,1]{2,1,0:T(8,128)S(1)}, f32[2,16,1]{2,1,0:T(8,128)S(1)}, u32[]{:S(2)}, u32[]{:S(2)}) collective-permute-start(f32[2,16,1]{2,1,0:T(8,128)S(1)} %get-tuple-element.119), channel_id=1, source_target_pairs={{0,1},{1,2},{2,3},{3,4},{4,5},{5,6},{6,7},{7,0},{8,9},{9,10},{10,1... | collective-permute-start | bytes 392 | tf_op jit(solution)/shard_map/ppermute | solution.py:26
  1463.8 31.7 %collective-permute-start.101 = (f32[2,1,64]{2,1,0:T(1,128)S(1)}, f32[2,1,64]{2,1,0:T(1,128)S(1)}, u32[]{:S(2)}, u32[]{:S(2)}) collective-permute-start(f32[2,1,64]{2,1,0:T(1,128)S(1)} %copy.2875), channel_id=1, source_target_pairs={{0,8},{8,16},{16,24},{24,0},{1,9},{9,17},{17,25},{25,1},{2,10},{10... | collective-permute-start | bytes 1544 | tf_op jit(solution)/shard_map/ppermute | solution.py:26
  1536.5 6.6 collective-permute-start.107
  1621.3 6.6 collective-permute-start.111
  (66 other events, 584.2 us)
where the time goes:
time: 1680 us; the launch traced here: 1670 us
  blocking collectives  1380 us (82%)
  starting transfers between devices  94.1 us (6%)
  local copies, waits for them, and re-layouts  83.3 us (5%)
  waiting for transfers between devices  77.8 us (5%)
  between operations  16.8 us (1%)
    all_gather x22, blocking collectives, operate(): lax.all_gather(field[:, 0, :], 'gx', axis=1, tiled=True)  538 us
    all_gather x22, blocking collectives, operate(): lax.all_gather(field[:, -1, :], 'gx', axis=1, tiled=True)  489 us
    psum x6, blocking collectives, total_inner(): return lax.psum(jnp.sum(first_field * second_field), ('gy', 'gx'))  231 us
    all_gather x4, blocking collectives, coarsest(): gathered = lax.all_gather(residual, 'gx', axis=2, tiled=True)  123 us
    ppermute x56, starting transfers between devices, padded(): lax.ppermute(head, axis, [((i + 1) % count, i) for i in range(count)])  86.9 us
    ppermute x56, waiting for transfers between devices, padded(): lax.ppermute(tail, axis, [(i, (i + 1) % count) for i in range(count)])  67.5 us
  transfers between devices with their start and end apart: 112, of which 33 were waited for; matrix products, arithmetic and copies ran while one was open for 4% of the time, Pallas kernels for 0%

commit v1 on v0

v1 whole, which is shorter than its diff:
```python
import jax
import jax.numpy as jnp
from jax import lax
from jax.experimental import pallas as pl
from jax.experimental.pallas import tpu as pltpu
from jax.sharding import PartitionSpec as P

STEPS = 2
ITERS = 2
LEVELS = 3
COARSE = 4

RELAXATION = 0.8
DIFFUSION = 4.0
VERTICAL = 1.0
REACTION = 0.5
ADVECTION = 0.5

LANES = 128
SUB = 8


class Level:
    def __init__(self, index, pages, strip_rows, strips, planes):
        self.pages = pages >> index
        self.rows = strip_rows >> index
        self.strips = strips
        self.planes = planes
        self.pitch = self.rows + SUB
        self.height = strips * self.pitch + SUB
        self.factor = 2**index
        self.coupling = DIFFUSION / 4.0**index
        self.diagonal = 1.0 + 4.0 * self.coupling + 2.0 * VERTICAL
        self.relax = RELAXATION / self.diagonal
        self.tiles = self.rows // SUB
        self.count = self.pages * planes

    def shape(self):
        return (self.count * self.height, LANES)

    def base(self, strip, tile):
        return pl.multiple_of(SUB + strip * self.pitch + tile * SUB, SUB)


def tile_of(ref, level, page, plane, row):
    return ref[pl.ds((page * level.planes + plane) * level.height + row, SUB), :]


def put_tile(ref, level, page, plane, row, value):
    ref[pl.ds((page * level.planes + plane) * level.height + row, SUB), :] = value


def fill_halo(ref, level, offsets, step, halo):
    count, width = level.count, level.pages
    for strip in range(level.strips):
        shift = offsets[step, strip] // level.factor
        lane, page = shift // width, shift % width
        under = (strip - 1) % level.strips
        first = SUB + strip * level.pitch
        last = SUB + under * level.pitch + level.rows - 1
        upper = ref[pl.ds(first, count, stride=level.height), :]
        lower = ref[pl.ds(last, count, stride=level.height), :]
        start = strip * 4 * count
        halo[pl.ds(start, count), :] = pltpu.roll(upper, (LANES - lane) % LANES, 1)
        halo[pl.ds(start + count, count), :] = pltpu.roll(upper, LANES - 1 - lane, 1)
        halo[pl.ds(start + 2 * count, count), :] = pltpu.roll(lower, (lane + 1) % LANES, 1)
        halo[pl.ds(start + 3 * count, count), :] = pltpu.roll(lower, lane, 1)
        ref[pl.ds(last + 1, count, stride=level.height), :] = halo[pl.ds(start + page * level.planes, count), :]
        ref[pl.ds(first - 1, count, stride=level.height), :] = halo[
            pl.ds(start + 2 * count + (width - page) * level.planes, count), :
        ]


def stencil(ref, level, base):
    planes, width = level.planes, level.pages
    cell = [[tile_of(ref, level, p, z, base) for z in range(planes)] for p in range(width)]
    out = []
    for p in range(width):
        row = []
        for z in range(planes):
            right = cell[p + 1][z] if p + 1 < width else pltpu.roll(cell[0][z], LANES - 1, 1)
            left = cell[p - 1][z] if p else pltpu.roll(cell[width - 1][z], 1, 1)
            above = tile_of(ref, level, p, z, base + 1)
            below = tile_of(ref, level, p, z, base - 1)
            beside = (above + below) + (right + left)
            vertical = cell[p][(z + 1) % planes] + cell[p][(z - 1) % planes]
            row.append((cell[p][z], right, left, beside, vertical))
        out.append(row)
    return out


def smooth(level, cell, beside, vertical):
    k = level.relax
    return (1.0 - k * level.diagonal) * cell + (k * level.coupling) * beside + (k * VERTICAL) * vertical


def apply(level, cell, beside, vertical):
    return level.diagonal * cell - level.coupling * beside - VERTICAL * vertical


def restrict(ref, level, coarse_ref, coarse, pairs):
    planes = level.planes

    def body(index, carry):
        strip, tile = index // coarse.tiles, index % coarse.tiles
        for half in range(2):
            base = level.base(strip, 2 * tile + half)
            terms = stencil(ref, level, base)
            for p in range(coarse.pages):
                for z in range(planes):
                    total = 0.0
                    for q in (2 * p, 2 * p + 1):
                        cell, _, _, beside, vertical = terms[q][z]
                        total = total + smooth(level, cell, beside, vertical)
                    pairs[pl.ds((p * planes + z) * 2 * SUB + half * SUB, SUB), :] = total
        for p in range(coarse.pages):
            for z in range(planes):
                start = (p * planes + z) * 2 * SUB
                even = pairs[pl.ds(start, SUB, stride=2), :]
                odd = pairs[pl.ds(start + 1, SUB, stride=2), :]
                put_tile(coarse_ref, coarse, p, z, coarse.base(strip, tile), 0.25 * (even + odd))
        return carry

    lax.fori_loop(0, coarse.strips * coarse.tiles, body, 0)


def prolong(coarse_ref, coarse, residual, level, ref, pairs):
    planes = level.planes

    def body(index, carry):
        strip, tile = index // coarse.tiles, index % coarse.tiles
        for p in range(coarse.pages):
            for z in range(planes):
                start = (p * planes + z) * 2 * SUB
                value = tile_of(coarse_ref, coarse, p, z, coarse.base(strip, tile))
                pairs[pl.ds(start, SUB, stride=2), :] = value
                pairs[pl.ds(start + 1, SUB, stride=2), :] = value
        for p in range(coarse.pages):
            for z in range(planes):
                start = (p * planes + z) * 2 * SUB
                for half in range(2):
                    value = pairs[pl.ds(start + half * SUB, SUB), :]
                    base = level.base(strip, 2 * tile + half)
                    for q in (2 * p, 2 * p + 1):
                        put_tile(ref, level, q, z, base, level.relax * tile_of(residual, level, q, z, base) + value)
        return carry

    lax.fori_loop(0, coarse.strips * coarse.tiles, body, 0)


def per_tile(level, body, sums):
    def step(index, carry):
        return body(level.base(index // level.tiles, index % level.tiles), carry)

    zero = jnp.zeros((SUB, LANES), jnp.float32)
    return lax.fori_loop(0, level.strips * level.tiles, step, (zero,) * sums)


def total(vector):
    return jnp.sum(jnp.sum(vector, axis=0, keepdims=True), axis=1, keepdims=True)


def relaxed(ref, residual, level, target):
    def body(base, carry):
        for p, row in enumerate(stencil(ref, level, base)):
            for z, (cell, _, _, beside, vertical) in enumerate(row):
                value = smooth(level, cell, beside, vertical) + level.relax * tile_of(residual, level, p, z, base)
                put_tile(target, level, p, z, base, value)
        return carry

    per_tile(level, body, 0)


def coarsest(residual, level, offsets, step, spare, halo):
    def first(base, carry):
        for p, row in enumerate(stencil(residual, level, base)):
            for z, (cell, _, _, beside, vertical) in enumerate(row):
                put_tile(spare[0], level, p, z, base, level.relax * (cell + smooth(level, cell, beside, vertical)))
        return carry

    fill_halo(residual, level, offsets, step, halo)
    per_tile(level, first, 0)
    now = 0
    for _ in range(COARSE - 2):
        fill_halo(spare[now], level, offsets, step, halo)
        relaxed(spare[now], residual, level, spare[1 - now])
        now = 1 - now
    return spare[now]


def vcycle(residual, levels, index, offsets, step, work, halo, pairs):
    level, coarse = levels[index], levels[index + 1]
    below, estimate = work[index + 1], work[index][1]
    fill_halo(residual, level, offsets, step, halo)
    restrict(residual, level, below[0], coarse, pairs)
    if index + 2 == LEVELS:
        correction = coarsest(below[0], coarse, offsets, step, below[1:], halo)
    else:
        vcycle(below[0], levels, index + 1, offsets, step, work, halo, pairs)
        correction = below[2]
        relaxed(below[1], below[0], coarse, correction)
    prolong(correction, coarse, residual, level, estimate, pairs)
    fill_halo(estimate, level, offsets, step, halo)


def interleave(ref, level):
    width, planes = level.pages, level.planes
    lane = lax.broadcasted_iota(jnp.int32, (SUB, LANES), 1)
    per = LANES // width
    source = (lane % per) * width + lane // per

    def body(index, carry):
        base = level.base(index // level.tiles, index % level.tiles)
        for z in range(planes):
            pages = [tile_of(ref, level, p, z, base) for p in range(width)]
            bit = 1
            while bit < width:
                low = (lane // bit) % 2 == 0
                for p in range(width):
                    if not p & bit:
                        a, b = pages[p], pages[p | bit]
                        pages[p] = jnp.where(low, a, pltpu.roll(b, bit, 1))
                        pages[p | bit] = jnp.where(low, pltpu.roll(a, LANES - bit, 1), b)
                bit *= 2
            for p in range(width):
                put_tile(ref, level, p, z, base, jnp.take_along_axis(pages[p], source, axis=1))
        return carry

    lax.fori_loop(0, level.strips * level.tiles, body, 0)


def solve(offsets, u, v, r, q, w, work, halo, pairs, levels):
    fine = levels[0]
    e = work[0][1]
    update = None
    for step in range(STEPS):
        fill_halo(u, fine, offsets, step, halo)

        def residual(base, carry):
            for p, row in enumerate(stencil(u, fine, base)):
                for z, (cell, right, left, beside, vertical) in enumerate(row):
                    speed = tile_of(v, fine, p, z, base)
                    cube = cell * cell * cell
                    value = (
                        (1.0 + REACTION - fine.diagonal) * cell
                        - REACTION * cube
                        - ADVECTION * speed * (right - left)
                        + fine.coupling * beside
                        + VERTICAL * vertical
                    )
                    put_tile(r, fine, p, z, base, value)
            return carry

        per_tile(fine, residual, 0)
        vcycle(r, levels, 0, offsets, step, work, halo, pairs)

        def finish(base, carry):
            (rw,) = carry
            for p, row in enumerate(stencil(e, fine, base)):
                for z, (cell, _, _, beside, vertical) in enumerate(row):
                    res = tile_of(r, fine, p, z, base)
                    value = smooth(fine, cell, beside, vertical) + fine.relax * res
                    put_tile(w, fine, p, z, base, value)
                    rw = rw + res * value
            return (rw,)

        (rw,) = per_tile(fine, finish, 1)
        rw = total(rw)
        fill_halo(w, fine, offsets, step, halo)

        def image(base, carry):
            (wq,) = carry
            for p, row in enumerate(stencil(w, fine, base)):
                for z, (cell, _, _, beside, vertical) in enumerate(row):
                    value = apply(fine, cell, beside, vertical)
                    put_tile(q, fine, p, z, base, value)
                    wq = wq + cell * value
            return (wq,)

        (wq,) = per_tile(fine, image, 1)
        alpha = rw / total(wq)
        vcycle(q, levels, 0, offsets, step, work, halo, pairs)

        def finish_next(base, carry):
            (rw,) = carry
            for p, row in enumerate(stencil(e, fine, base)):
                for z, (cell, _, _, beside, vertical) in enumerate(row):
                    img = tile_of(q, fine, p, z, base)
                    value = smooth(fine, cell, beside, vertical) + fine.relax * img
                    res = tile_of(r, fine, p, z, base) - alpha * img
                    value = tile_of(w, fine, p, z, base) - alpha * value
                    put_tile(r, fine, p, z, base, value)
                    rw = rw + res * value
            return (rw,)

        (following,) = per_tile(fine, finish_next, 1)
        following = total(following)
        beta = following / rw
        fill_halo(r, fine, offsets, step, halo)

        def image_next(base, carry):
            (pq,) = carry
            for p, row in enumerate(stencil(r, fine, base)):
                for z, (cell, _, _, beside, vertical) in enumerate(row):
                    direction = cell + beta * tile_of(w, fine, p, z, base)
                    value = apply(fine, cell, beside, vertical) + beta * tile_of(q, fine, p, z, base)
                    pq = pq + direction * value
            return (pq,)

        (pq,) = per_tile(fine, image_next, 1)
        alpha_next = following / total(pq)
        along = alpha + alpha_next * beta

        def update(base, carry):
            for p in range(fine.pages):
                for z in range(fine.planes):
                    value = (
                        tile_of(u, fine, p, z, base)
                        + along * tile_of(w, fine, p, z, base)
                        + alpha_next * tile_of(r, fine, p, z, base)
                    )
                    put_tile(u, fine, p, z, base, value)
            return carry

        if step + 1 < STEPS:
            per_tile(fine, update, 0)
    return update


def whole_kernel(keys, levels, *refs):
    count = len(keys)
    offsets, blocks, out = refs[0], refs[1 : 1 + count], refs[1 + count]
    u, v, r, q, w, e, r1, e1, f1, r2, e2, f2, halo, pairs, sems = refs[2 + count :]
    fine = levels[0]
    gy, gx = lax.axis_index("gy"), lax.axis_index("gx")
    copies = []
    for index, (name, dy, dx) in enumerate(keys):
        target = u if name == "u" else v
        row = SUB + jnp.bitwise_xor(gy, dy) * fine.pitch
        for z in range(fine.planes):
            start = (jnp.bitwise_xor(gx, dx) * fine.planes + z) * fine.height + row
            copy = pltpu.make_async_copy(
                blocks[index].at[z],
                target.at[pl.ds(pl.multiple_of(start, SUB), fine.rows), :],
                sems.at[index * fine.planes + z],
            )
            copy.start()
            copies.append(copy)
    for copy in copies:
        copy.wait()
    interleave(u, fine)
    interleave(v, fine)
    work = [[r, e], [r1, e1, f1], [r2, e2, f2]]
    update = solve(offsets, u, v, r, q, w, work, halo, pairs, levels)
    lane = lax.broadcasted_iota(jnp.int32, (SUB, LANES), 1)
    source = gx * (LANES // fine.pages) + lane // fine.pages
    for tile in range(fine.tiles):
        base = fine.base(gy, tile)
        update(base, ())
        for z in range(fine.planes):
            value = jnp.zeros((SUB, LANES), jnp.float32)
            for p in range(fine.pages):
                page = jnp.take_along_axis(tile_of(u, fine, p, z, base), source, axis=1)
                value = jnp.where(lane % fine.pages == p, page, value)
            out[z, pl.ds(tile * SUB, SUB), :] = value


def on_whole(blocks, offsets, strips, width):
    keys = sorted(blocks)
    planes, rows, columns = blocks[keys[0]].shape
    levels = [Level(i, width, rows, strips, planes) for i in range(LEVELS)]
    fields = [pltpu.VMEM(levels[0].shape(), jnp.float32)] * 6
    fields += [pltpu.VMEM(levels[1].shape(), jnp.float32)] * 3 + [pltpu.VMEM(levels[2].shape(), jnp.float32)] * 3
    count = levels[0].count
    scratch = fields + [
        pltpu.VMEM((strips * 4 * count, LANES), jnp.float32),
        pltpu.VMEM((count * SUB, LANES), jnp.float32),
        pltpu.SemaphoreType.DMA((len(keys) * planes,)),
    ]

    def kernel(*refs):
        whole_kernel(keys, levels, *refs)

    return pl.pallas_call(
        kernel,
        out_shape=jax.ShapeDtypeStruct((planes, rows, columns), jnp.float32),
        in_specs=[pl.BlockSpec(memory_space=pltpu.SMEM)] + [pl.BlockSpec(memory_space=pl.ANY)] * len(keys),
        out_specs=pl.BlockSpec(memory_space=pltpu.VMEM),
        scratch_shapes=scratch,
        compiler_params=pltpu.CompilerParams(vmem_limit_bytes=48 << 20),
    )(offsets, *[blocks[key] for key in keys])


def swapped(block, axis, bits):
    count = lax.axis_size(axis)
    return lax.ppermute(block, axis, [(i, i ^ bits) for i in range(count)])


def gathered(phase, velocity):
    out = {}
    for name, own in (("u", phase), ("v", velocity)):
        out[name, 0, 0] = own
        for k in (2, 4, 6):
            out[name, 0, k] = swapped(own, "gx", k)
        for k in (0, 2, 4, 6):
            out[name, 0, k | 1] = swapped(out[name, 0, k], "gx", 1)
            out[name, 2, k] = swapped(out[name, 0, k], "gy", 2)
            out[name, 2, k | 1] = swapped(out[name, 2, k], "gx", 1)
    for (name, dy, dx), block in list(out.items()):
        out[name, dy ^ 1, dx] = swapped(block, "gy", 1)
    return out


def padded(cells, sides, width):
    for axis, dim in sides:
        count = lax.axis_size(axis)
        head = lax.slice_in_dim(cells, 0, width, axis=dim)
        tail = lax.slice_in_dim(cells, cells.shape[dim] - width, cells.shape[dim], axis=dim)
        cells = jnp.concatenate(
            [
                lax.ppermute(tail, axis, [(i, (i + 1) % count) for i in range(count)]),
                cells,
                lax.ppermute(head, axis, [((i + 1) % count, i) for i in range(count)]),
            ],
            axis=dim,
        )
    return cells


def sheared(bottom_row, upper_row, offsets_now, anchor, columns):
    breadth = bottom_row.shape[1]
    device_row = lax.axis_index("gy")
    row_count = lax.axis_size("gy")
    below_shift = offsets_now[device_row]
    above_shift = offsets_now[(device_row + 1) % row_count]
    local_columns = jnp.arange(columns, dtype=jnp.int32)
    down_index = (anchor + below_shift + local_columns) % breadth
    up_index = (anchor - above_shift + local_columns) % breadth
    down_window = jnp.take(bottom_row, down_index, axis=1)
    up_window = jnp.take(upper_row, up_index, axis=1)
    stacked = jnp.stack([down_window, up_window], axis=1)
    rims = padded(stacked, (("gy", 1),), 1)
    return (rims[:, 0, :], rims[:, 3, :])


def block_stencil(field, below_row, above_row, across, coupling):
    diagonal = 1.0 + 4.0 * coupling + 2.0 * VERTICAL
    column_pad = jnp.concatenate([below_row[:, None, :], field, above_row[:, None, :]], axis=1)
    beside = column_pad[:, 2:, :] + column_pad[:, :-2, :] + across
    vertical_sum = jnp.roll(field, 1, 0) + jnp.roll(field, -1, 0)
    return diagonal * field - coupling * beside - VERTICAL * vertical_sum


def block_operate(field, offsets_now, coupling):
    columns = field.shape[2]
    margins = padded(field, (("gx", 2),), 1)
    bottom_full, upper_full = (
        lax.all_gather(field[:, 0, :], "gx", axis=1, tiled=True),
        lax.all_gather(field[:, -1, :], "gx", axis=1, tiled=True),
    )
    right_field = margins[:, :, 2:]
    left_field = margins[:, :, :-2]
    below_row, above_row = sheared(
        bottom_full, upper_full, offsets_now, lax.axis_index("gx") * columns, columns
    )
    across = right_field + left_field
    return (block_stencil(field, below_row, above_row, across, coupling), right_field, left_field)


def block_operate_strip(field, offsets_now, coupling):
    below_row, above_row = sheared(field[:, 0, :], field[:, -1, :], offsets_now, 0, field.shape[2])
    across = jnp.roll(field, 1, 2) + jnp.roll(field, -1, 2)
    return block_stencil(field, below_row, above_row, across, coupling)


def block_coarsest(residual, offsets_now, coupling):
    diagonal = 1.0 + 4.0 * coupling + 2.0 * VERTICAL
    columns = residual.shape[2]
    gathered = lax.all_gather(residual, "gx", axis=2, tiled=True)
    estimate = RELAXATION * gathered / diagonal
    for sweep_index in range(COARSE - 1):
        estimate = (
            estimate
            + RELAXATION * (gathered - block_operate_strip(estimate, offsets_now, coupling)) / diagonal
        )
    return lax.dynamic_slice_in_dim(estimate, lax.axis_index("gx") * columns, columns, 2)


def block_vcycle(residual, offsets_raw, layer_index):
    factor = 2**layer_index
    coupling = DIFFUSION / 4.0**layer_index
    diagonal = 1.0 + 4.0 * coupling + 2.0 * VERTICAL
    offsets_now = offsets_raw // factor
    if layer_index == LEVELS - 1:
        return block_coarsest(residual, offsets_now, coupling)
    estimate = RELAXATION * residual / diagonal
    defect = residual - block_operate(estimate, offsets_now, coupling)[0]
    planes, height, breadth = defect.shape
    coarser = defect.reshape(planes, height // 2, 2, breadth // 2, 2).mean(axis=(2, 4))
    correction = block_vcycle(coarser, offsets_raw, layer_index + 1)
    estimate = estimate + jnp.repeat(jnp.repeat(correction, 2, axis=1), 2, axis=2)
    estimate = (
        estimate + RELAXATION * (residual - block_operate(estimate, offsets_now, coupling)[0]) / diagonal
    )
    return estimate


def total_inner(first_field, second_field):
    return lax.psum(jnp.sum(first_field * second_field), ("gy", "gx"))


def spread(phase, velocity, offsets):
    phase_now = phase
    for time_step in range(STEPS):
        offsets_raw = offsets[time_step]
        applied, right_field, left_field = block_operate(phase_now, offsets_raw, DIFFUSION)
        source = (
            phase_now
            + REACTION * (phase_now - phase_now * phase_now * phase_now)
            - ADVECTION * velocity * (right_field - left_field)
        )
        residual = source - applied
        precond = block_vcycle(residual, offsets_raw, 0)
        projected = total_inner(residual, precond)
        direction = precond
        for iteration in range(ITERS):
            image = block_operate(direction, offsets_raw, DIFFUSION)[0]
            step_size = projected / total_inner(direction, image)
            phase_now = phase_now + step_size * direction
            residual = residual - step_size * image
            if iteration + 1 < ITERS:
                precond = block_vcycle(residual, offsets_raw, 0)
                following = total_inner(residual, precond)
                direction = precond + following / projected * direction
                projected = following
    return phase_now


MOST_DEVICES = 32
MOST_BYTES = 44 << 20


def local(phase, velocity, offsets):
    strips, width = lax.axis_size("gy"), lax.axis_size("gx")
    planes, rows, columns = phase.shape
    sizes = Level(0, width, rows, strips, planes).shape()
    fits = 8 * 4 * sizes[0] * sizes[1] < MOST_BYTES and strips * width <= MOST_DEVICES
    shaped = columns == LANES and rows % 32 == 0 and width in (8, 16, 32, 64) and strips % 4 == 0
    if fits and shaped:
        return on_whole(gathered(phase, velocity), offsets, strips, width)
    return spread(phase, velocity, offsets)


def solution(mesh):
    placed = (P(None, "gy", "gx"), P(None, "gy", "gx"), P())
    return jax.shard_map(local, mesh=mesh, in_specs=placed, out_specs=P(None, "gy", "gx"), check_vma=False)
```

time: 1680 us -> 104 us (0.06)
  blocking collectives: 1380 us -> 0 us
  local copies, waits for them, and re-layouts: 83.3 us -> 2.19 us
  waiting for transfers between devices: 77.8 us -> 13 us
  starting transfers between devices: 94.1 us -> 41.3 us
  Pallas kernels: 0 us -> 46.9 us
    all_gather x48 -> x0, blocking collectives: 1150 us -> none  [the longest x22 538 us: operate(): lax.all_gather(field[:, 0, :], 'gx', axis=1, tiled=True)]
    psum x6 -> x0, blocking collectives: 231 us -> none  [total_inner(): return lax.psum(jnp.sum(first_field * second_field), ('gy', 'gx'))]
    ppermute x112 -> x62, waiting for transfers between devices: 77.8 us -> 13 us  [swapped(): return lax.ppermute(block, axis, [(i, i ^ bits) for i in range(count)])]
    ppermute x112 -> x62, starting transfers between devices: 94.1 us -> 41.3 us  [swapped(): return lax.ppermute(block, axis, [(i, i ^ bits) for i in range(count)])]
    gather x120 -> x0, local copies, waits for them, and re-layouts: 48.8 us -> none  [the longest x60 24.4 us: sheared(): down_window = jnp.take(bottom_row, down_index, axis=1)]
    pallas_call x0 -> x1, Pallas kernels: none -> 46.9 us  [on_whole(): pl.pallas_call(kernel, out_shape=jax.ShapeDtypeStruct((planes, rows, colu...]
  transfers between devices with their start and end apart: 112 -> 62, of which waited for: 33 -> 17; matrix products, arithmetic and copies ran while one was open for 4% -> 0% of each run, Pallas kernels for 0% -> 0%
where the time goes in v1:
time: 104 us; the launch traced here: 103 us
  Pallas kernels  46.9 us (45%)
  starting transfers between devices  41.3 us (40%)
  waiting for transfers between devices  13 us (12%)
  local copies, waits for them, and re-layouts  2.19 us (2%)
    pallas_call x1, Pallas kernels, on_whole(): pl.pallas_call(kernel, out_shape=jax.ShapeDtypeStruct((planes, rows, colu...  46.9 us
    ppermute x62, starting transfers between devices, swapped(): return lax.ppermute(block, axis, [(i, i ^ bits) for i in range(count)])  41.3 us
    ppermute x62, waiting for transfers between devices, swapped(): return lax.ppermute(block, axis, [(i, i ^ bits) for i in range(count)])  13 us
    unnamed x6, local copies, waits for them, and re-layouts  2.19 us
  transfers between devices with their start and end apart: 62, of which 17 were waited for; matrix products, arithmetic and copies ran while one was open for 0% of the time, Pallas kernels for 0%

profile of v1, /device:TPU:0, one launch (start us, length us, event | category | flops | bytes accessed | tf_op | source)
XLA Modules:
  0.0 103.4 jit_solution(12997196539860897112)
XLA Ops:
  0.0 0.5 collective-permute-start.7
  0.5 4.6 %collective-permute-start.5 = (f32[2,32,128]{2,1,0:T(8,128)}, f32[2,32,128]{2,1,0:T(8,128)S(1)}, u32[]{:S(2)}, u32[]{:S(2)}) collective-permute-start(f32[2,32,128]{2,1,0:T(8,128)} %refs_1_.1), channel_id=1, source_target_pairs={{0,6},{1,7},{2,4},{3,5},{4,2},{5,3},{6,0},{7,1},{8,14},{9,15},{10,... | collective-permute-start | bytes 98312 | tf_op jit(solution)/shard_map/ppermute | solution.py:396
  5.1 0.6 collective-permute-start.1
  5.7 1.6 %collective-permute-start = (f32[2,32,128]{2,1,0:T(8,128)}, f32[2,32,128]{2,1,0:T(8,128)S(1)}, u32[]{:S(2)}, u32[]{:S(2)}) collective-permute-start(f32[2,32,128]{2,1,0:T(8,128)} %refs_1_.1), channel_id=1, source_target_pairs={{0,1},{1,0},{2,3},{3,2},{4,5},{5,4},{6,7},{7,6},{8,9},{9,8},{10,11... | collective-permute-start | bytes 98312 | tf_op jit(solution)/shard_map/ppermute | solution.py:396
  7.4 1.5 %collective-permute-start.15 = (f32[2,32,128]{2,1,0:T(8,128)}, f32[2,32,128]{2,1,0:T(8,128)S(1)}, u32[]{:S(2)}, u32[]{:S(2)}) collective-permute-start(f32[2,32,128]{2,1,0:T(8,128)} %refs_1_.1), channel_id=1, source_target_pairs={{0,16},{8,24},{16,0},{24,8},{1,17},{9,25},{17,1},{25,9},{2,18},{10... | collective-permute-start | bytes 98312 | tf_op jit(solution)/shard_map/ppermute | solution.py:396
  8.9 1.2 %collective-permute-done.3.refs_5_ = f32[2,32,128]{2,1,0:T(8,128)S(1)} collective-permute-done((f32[2,32,128]{2,1,0:T(8,128)}, f32[2,32,128]{2,1,0:T(8,128)S(1)}, u32[]{:S(2)}, u32[]{:S(2)}) %collective-permute-start.3) | collective-permute-done | bytes 32800 | tf_op jit(solution)/shard_map/ppermute | solution.py:396
  10.1 2.5 %collective-permute-start.36 = (f32[2,32,128]{2,1,0:T(8,128)}, f32[2,32,128]{2,1,0:T(8,128)S(1)}, u32[]{:S(2)}, u32[]{:S(2)}) collective-permute-start(f32[2,32,128]{2,1,0:T(8,128)} %refs_33_.1), channel_id=1, source_target_pairs={{0,6},{1,7},{2,4},{3,5},{4,2},{5,3},{6,0},{7,1},{8,14},{9,15},{10,... | collective-permute-start | bytes 98312 | tf_op jit(solution)/shard_map/ppermute | solution.py:396
  12.6 1.9 %collective-permute-start.32 = (f32[2,32,128]{2,1,0:T(8,128)}, f32[2,32,128]{2,1,0:T(8,128)S(1)}, u32[]{:S(2)}, u32[]{:S(2)}) collective-permute-start(f32[2,32,128]{2,1,0:T(8,128)} %refs_33_.1), channel_id=1, source_target_pairs={{0,2},{1,3},{2,0},{3,1},{4,6},{5,7},{6,4},{7,5},{8,10},{9,11},{10,... | collective-permute-start | bytes 98312 | tf_op jit(solution)/shard_map/ppermute | solution.py:396
  14.5 1.5 %collective-permute-start.31 = (f32[2,32,128]{2,1,0:T(8,128)}, f32[2,32,128]{2,1,0:T(8,128)S(1)}, u32[]{:S(2)}, u32[]{:S(2)}) collective-permute-start(f32[2,32,128]{2,1,0:T(8,128)} %refs_33_.1), channel_id=1, source_target_pairs={{0,1},{1,0},{2,3},{3,2},{4,5},{5,4},{6,7},{7,6},{8,9},{9,8},{10,11... | collective-permute-start | bytes 98312 | tf_op jit(solution)/shard_map/ppermute | solution.py:396
  16.0 1.5 %collective-permute-start.46 = (f32[2,32,128]{2,1,0:T(8,128)}, f32[2,32,128]{2,1,0:T(8,128)S(1)}, u32[]{:S(2)}, u32[]{:S(2)}) collective-permute-start(f32[2,32,128]{2,1,0:T(8,128)} %refs_33_.1), channel_id=1, source_target_pairs={{0,16},{8,24},{16,0},{24,8},{1,17},{9,25},{17,1},{25,9},{2,18},{10... | collective-permute-start | bytes 98312 | tf_op jit(solution)/shard_map/ppermute | solution.py:396
  17.5 0.5 collective-permute-start.21
  18.0 1.1 %collective-permute-start.6 = (f32[2,32,128]{2,1,0:T(8,128)S(1)}, f32[2,32,128]{2,1,0:T(8,128)S(1)}, u32[]{:S(2)}, u32[]{:S(2)}) collective-permute-start(f32[2,32,128]{2,1,0:T(8,128)S(1)} %collective-permute-done.5.refs_7_), channel_id=1, source_target_pairs={{0,1},{1,0},{2,3},{3,2},{4,5},{5,4},{6,7},{7,6},{8,9},{9,8},{10,11... | collective-permute-start | bytes 98312 | tf_op jit(solution)/shard_map/ppermute | solution.py:396
  19.1 1.0 %collective-permute-start.19 = (f32[2,32,128]{2,1,0:T(8,128)S(1)}, f32[2,32,128]{2,1,0:T(8,128)S(1)}, u32[]{:S(2)}, u32[]{:S(2)}) collective-permute-start(f32[2,32,128]{2,1,0:T(8,128)S(1)} %collective-permute-done.3.refs_5_), channel_id=1, source_target_pairs={{0,16},{8,24},{16,0},{24,8},{1,17},{9,25},{17,1},{25,9},{2,18},{10... | collective-permute-start | bytes 98312 | tf_op jit(solution)/shard_map/ppermute | solution.py:396
  20.2 1.3 %collective-permute-done.21.refs_23_ = f32[2,32,128]{2,1,0:T(8,128)S(1)} collective-permute-done((f32[2,32,128]{2,1,0:T(8,128)S(1)}, f32[2,32,128]{2,1,0:T(8,128)S(1)}, u32[]{:S(2)}, u32[]{:S(2)}) %collective-permute-start.21) | collective-permute-done | bytes 32800 | tf_op jit(solution)/shard_map/ppermute | solution.py:396
  21.4 0.5 collective-permute-start.4
  22.0 1.0 collective-permute-start.17
  23.0 1.1 %collective-permute-start.2 = (f32[2,32,128]{2,1,0:T(8,128)S(1)}, f32[2,32,128]{2,1,0:T(8,128)S(1)}, u32[]{:S(2)}, u32[]{:S(2)}) collective-permute-start(f32[2,32,128]{2,1,0:T(8,128)S(1)} %collective-permute-done.1.refs_3_), channel_id=1, source_target_pairs={{0,1},{1,0},{2,3},{3,2},{4,5},{5,4},{6,7},{7,6},{8,9},{9,8},{10,11... | collective-permute-start | bytes 98312 | tf_op jit(solution)/shard_map/ppermute | solution.py:396
  24.3 1.1 %collective-permute-done.4.refs_6_ = f32[2,32,128]{2,1,0:T(8,128)S(1)} collective-permute-done((f32[2,32,128]{2,1,0:T(8,128)S(1)}, f32[2,32,128]{2,1,0:T(8,128)S(1)}, u32[]{:S(2)}, u32[]{:S(2)}) %collective-permute-start.4) | collective-permute-done | bytes 32800 | tf_op jit(solution)/shard_map/ppermute | solution.py:396
  25.4 0.5 collective-permute-done.17.refs_19_
  25.9 1.5 %collective-permute-start.16 = (f32[2,32,128]{2,1,0:T(8,128)S(1)}, f32[2,32,128]{2,1,0:T(8,128)S(1)}, u32[]{:S(2)}, u32[]{:S(2)}) collective-permute-start(f32[2,32,128]{2,1,0:T(8,128)S(1)} %collective-permute-done.15.refs_17_), channel_id=1, source_target_pairs={{0,1},{1,0},{2,3},{3,2},{4,5},{5,4},{6,7},{7,6},{8,9},{9,8},{10,11... | collective-permute-start | bytes 98312 | tf_op jit(solution)/shard_map/ppermute | solution.py:396
  27.4 0.6 collective-permute-start.52
  28.0 1.0 collective-permute-start.37
  29.0 1.0 %collective-permute-start.50 = (f32[2,32,128]{2,1,0:T(8,128)S(1)}, f32[2,32,128]{2,1,0:T(8,128)S(1)}, u32[]{:S(2)}, u32[]{:S(2)}) collective-permute-start(f32[2,32,128]{2,1,0:T(8,128)S(1)} %collective-permute-done.34.refs_37_), channel_id=1, source_target_pairs={{0,16},{8,24},{16,0},{24,8},{1,17},{9,25},{17,1},{25,9},{2,18},{10... | collective-permute-start | bytes 98312 | tf_op jit(solution)/shard_map/ppermute | solution.py:396
  30.0 1.3 %collective-permute-done.52.refs_55_ = f32[2,32,128]{2,1,0:T(8,128)S(1)} collective-permute-done((f32[2,32,128]{2,1,0:T(8,128)S(1)}, f32[2,32,128]{2,1,0:T(8,128)S(1)}, u32[]{:S(2)}, u32[]{:S(2)}) %collective-permute-start.52) | collective-permute-done | bytes 32800 | tf_op jit(solution)/shard_map/ppermute | solution.py:396
  31.3 0.5 collective-permute-start.35
  31.8 1.0 collective-permute-start.48
  32.9 1.1 %collective-permute-start.33 = (f32[2,32,128]{2,1,0:T(8,128)S(1)}, f32[2,32,128]{2,1,0:T(8,128)S(1)}, u32[]{:S(2)}, u32[]{:S(2)}) collective-permute-start(f32[2,32,128]{2,1,0:T(8,128)S(1)} %collective-permute-done.32.refs_35_), channel_id=1, source_target_pairs={{0,1},{1,0},{2,3},{3,2},{4,5},{5,4},{6,7},{7,6},{8,9},{9,8},{10,11... | collective-permute-start | bytes 98312 | tf_op jit(solution)/shard_map/ppermute | solution.py:396
  34.1 1.1 %collective-permute-done.35.refs_38_ = f32[2,32,128]{2,1,0:T(8,128)S(1)} collective-permute-done((f32[2,32,128]{2,1,0:T(8,128)S(1)}, f32[2,32,128]{2,1,0:T(8,128)S(1)}, u32[]{:S(2)}, u32[]{:S(2)}) %collective-permute-start.35) | collective-permute-done | bytes 32800 | tf_op jit(solution)/shard_map/ppermute | solution.py:396
  35.2 0.5 collective-permute-done.48.refs_51_
  35.8 1.5 %collective-permute-start.47 = (f32[2,32,128]{2,1,0:T(8,128)S(1)}, f32[2,32,128]{2,1,0:T(8,128)S(1)}, u32[]{:S(2)}, u32[]{:S(2)}) collective-permute-start(f32[2,32,128]{2,1,0:T(8,128)S(1)} %collective-permute-done.46.refs_49_), channel_id=1, source_target_pairs={{0,1},{1,0},{2,3},{3,2},{4,5},{5,4},{6,7},{7,6},{8,9},{9,8},{10,11... | collective-permute-start | bytes 98312 | tf_op jit(solution)/shard_map/ppermute | solution.py:396
  37.3 0.6 collective-permute-start.22
  38.0 0.4 collective-permute-start.27
  38.4 1.3 %collective-permute-done.47.refs_50_ = f32[2,32,128]{2,1,0:T(8,128)S(1)} collective-permute-done((f32[2,32,128]{2,1,0:T(8,128)S(1)}, f32[2,32,128]{2,1,0:T(8,128)S(1)}, u32[]{:S(2)}, u32[]{:S(2)}) %collective-permute-start.47) | collective-permute-done | bytes 32800 | tf_op jit(solution)/shard_map/ppermute | solution.py:396
  39.7 1.8 %collective-permute-start.20 = (f32[2,32,128]{2,1,0:T(8,128)S(1)}, f32[2,32,128]{2,1,0:T(8,128)S(1)}, u32[]{:S(2)}, u32[]{:S(2)}) collective-permute-start(f32[2,32,128]{2,1,0:T(8,128)S(1)} %collective-permute-done.19.refs_21_), channel_id=1, source_target_pairs={{0,1},{1,0},{2,3},{3,2},{4,5},{5,4},{6,7},{7,6},{8,9},{9,8},{10,11... | collective-permute-start | bytes 98312 | tf_op jit(solution)/shard_map/ppermute | solution.py:396
  41.4 0.5 collective-permute-start.25
  42.2 1.4 %collective-permute-done.20.refs_22_ = f32[2,32,128]{2,1,0:T(8,128)S(1)} collective-permute-done((f32[2,32,128]{2,1,0:T(8,128)S(1)}, f32[2,32,128]{2,1,0:T(8,128)S(1)}, u32[]{:S(2)}, u32[]{:S(2)}) %collective-permute-start.20) | collective-permute-done | bytes 32800 | tf_op jit(solution)/shard_map/ppermute | solution.py:396
  43.6 0.5 collective-permute-start.60
  44.1 2.1 %collective-permute-start.53 = (f32[2,32,128]{2,1,0:T(8,128)S(1)}, f32[2,32,128]{2,1,0:T(8,128)S(1)}, u32[]{:S(2)}, u32[]{:S(2)}) collective-permute-start(f32[2,32,128]{2,1,0:T(8,128)S(1)} %collective-permute-done.52.refs_55_), channel_id=1, source_target_pairs={{0,1},{1,0},{2,3},{3,2},{4,5},{5,4},{6,7},{7,6},{8,9},{9,8},{10,11... | collective-permute-start | bytes 98312 | tf_op jit(solution)/shard_map/ppermute | solution.py:396
  46.2 0.5 collective-permute-start.58
  46.9 1.2 %collective-permute-done.53.refs_56_ = f32[2,32,128]{2,1,0:T(8,128)S(1)} collective-permute-done((f32[2,32,128]{2,1,0:T(8,128)S(1)}, f32[2,32,128]{2,1,0:T(8,128)S(1)}, u32[]{:S(2)}, u32[]{:S(2)}) %collective-permute-start.53) | collective-permute-done | bytes 32800 | tf_op jit(solution)/shard_map/ppermute | solution.py:396
  48.1 2.3 %collective-permute-start.49 = (f32[2,32,128]{2,1,0:T(8,128)S(1)}, f32[2,32,128]{2,1,0:T(8,128)S(1)}, u32[]{:S(2)}, u32[]{:S(2)}) collective-permute-start(f32[2,32,128]{2,1,0:T(8,128)S(1)} %collective-permute-done.48.refs_51_), channel_id=1, source_target_pairs={{0,1},{1,0},{2,3},{3,2},{4,5},{5,4},{6,7},{7,6},{8,9},{9,8},{10,11... | collective-permute-start | bytes 98312 | tf_op jit(solution)/shard_map/ppermute | solution.py:396
  51.4 1.0 collective-permute-done.49.refs_52_
  52.4 0.5 collective-permute-start.61
  53.0 0.4 collective-permute-start.57
  54.3 0.8 copy-done
  55.1 0.8 copy-done.1
  55.9 0.7 copy-done.2
  56.5 46.9 %shard_map.37 = f32[2,32,128]{2,1,0:T(8,128)} custom-call(s32[2,4]{1,0:T(2,128)S(1)} %copy-done.2, f32[2,32,128]{2,1,0:T(8,128)S(1)} %copy-done, f32[2,32,128]{2,1,0:T(8,128)S(1)} %collective-permute-done.refs_2_, f32[2,32,128]{2,1,0:T(8,128)S(1)} %collective-permute-done.1.refs_3_, f32[2,32,128]{2,1,0:T(8,128)S(1)} %collective-permute-done.2.refs_4_, ...), custom_call_target="tpu_custom_call" | custom-call | tf_op jit(solution)/shard_map/pallas_call | solution.py:384
  (83 shorter events, 3.2 us)
Async XLA Ops:
  0.0 7.4 %collective-permute-start.7 = (f32[2,32,128]{2,1,0:T(8,128)}, f32[2,32,128]{2,1,0:T(8,128)S(1)}, u32[]{:S(2)}, u32[]{:S(2)}) collective-permute-start(f32[2,32,128]{2,1,0:T(8,128)} %refs_1_.1), channel_id=1, source_target_pairs={{0,8},{8,0},{16,24},{24,16},{1,9},{9,1},{17,25},{25,17},{2,10},{10... | collective-permute-start | bytes 98312 | tf_op jit(solution)/shard_map/ppermute | solution.py:396
  0.5 8.4 %collective-permute-start.5 = (f32[2,32,128]{2,1,0:T(8,128)}, f32[2,32,128]{2,1,0:T(8,128)S(1)}, u32[]{:S(2)}, u32[]{:S(2)}) collective-permute-start(f32[2,32,128]{2,1,0:T(8,128)} %refs_1_.1), channel_id=1, source_target_pairs={{0,6},{1,7},{2,4},{3,5},{4,2},{5,3},{6,0},{7,1},{8,14},{9,15},{10,... | collective-permute-start | bytes 98312 | tf_op jit(solution)/shard_map/ppermute | solution.py:396
  5.1 5.0 %collective-permute-start.3 = (f32[2,32,128]{2,1,0:T(8,128)}, f32[2,32,128]{2,1,0:T(8,128)S(1)}, u32[]{:S(2)}, u32[]{:S(2)}) collective-permute-start(f32[2,32,128]{2,1,0:T(8,128)} %refs_1_.1), channel_id=1, source_target_pairs={{0,4},{1,5},{2,6},{3,7},{4,0},{5,1},{6,2},{7,3},{8,12},{9,13},{10,... | collective-permute-start | bytes 98312 | tf_op jit(solution)/shard_map/ppermute | solution.py:396
  5.1 7.5 %collective-permute-start.1 = (f32[2,32,128]{2,1,0:T(8,128)}, f32[2,32,128]{2,1,0:T(8,128)S(1)}, u32[]{:S(2)}, u32[]{:S(2)}) collective-permute-start(f32[2,32,128]{2,1,0:T(8,128)} %refs_1_.1), channel_id=1, source_target_pairs={{0,2},{1,3},{2,0},{3,1},{4,6},{5,7},{6,4},{7,5},{8,10},{9,11},{10,... | collective-permute-start | bytes 98312 | tf_op jit(solution)/shard_map/ppermute | solution.py:396
  5.7 6.9 %collective-permute-start = (f32[2,32,128]{2,1,0:T(8,128)}, f32[2,32,128]{2,1,0:T(8,128)S(1)}, u32[]{:S(2)}, u32[]{:S(2)}) collective-permute-start(f32[2,32,128]{2,1,0:T(8,128)} %refs_1_.1), channel_id=1, source_target_pairs={{0,1},{1,0},{2,3},{3,2},{4,5},{5,4},{6,7},{7,6},{8,9},{9,8},{10,11... | collective-permute-start | bytes 98312 | tf_op jit(solution)/shard_map/ppermute | solution.py:396
  7.4 7.1 %collective-permute-start.15 = (f32[2,32,128]{2,1,0:T(8,128)}, f32[2,32,128]{2,1,0:T(8,128)S(1)}, u32[]{:S(2)}, u32[]{:S(2)}) collective-permute-start(f32[2,32,128]{2,1,0:T(8,128)} %refs_1_.1), channel_id=1, source_target_pairs={{0,16},{8,24},{16,0},{24,8},{1,17},{9,25},{17,1},{25,9},{2,18},{10... | collective-permute-start | bytes 98312 | tf_op jit(solution)/shard_map/ppermute | solution.py:396
  8.9 7.1 %collective-permute-start.38 = (f32[2,32,128]{2,1,0:T(8,128)}, f32[2,32,128]{2,1,0:T(8,128)S(1)}, u32[]{:S(2)}, u32[]{:S(2)}) collective-permute-start(f32[2,32,128]{2,1,0:T(8,128)} %refs_33_.1), channel_id=1, source_target_pairs={{0,8},{8,0},{16,24},{24,16},{1,9},{9,1},{17,25},{25,17},{2,10},{10... | collective-permute-start | bytes 98312 | tf_op jit(solution)/shard_map/ppermute | solution.py:396
  10.1 7.4 %collective-permute-start.36 = (f32[2,32,128]{2,1,0:T(8,128)}, f32[2,32,128]{2,1,0:T(8,128)S(1)}, u32[]{:S(2)}, u32[]{:S(2)}) collective-permute-start(f32[2,32,128]{2,1,0:T(8,128)} %refs_33_.1), channel_id=1, source_target_pairs={{0,6},{1,7},{2,4},{3,5},{4,2},{5,3},{6,0},{7,1},{8,14},{9,15},{10,... | collective-permute-start | bytes 98312 | tf_op jit(solution)/shard_map/ppermute | solution.py:396
  12.6 5.5 %collective-permute-start.34 = (f32[2,32,128]{2,1,0:T(8,128)}, f32[2,32,128]{2,1,0:T(8,128)S(1)}, u32[]{:S(2)}, u32[]{:S(2)}) collective-permute-start(f32[2,32,128]{2,1,0:T(8,128)} %refs_33_.1), channel_id=1, source_target_pairs={{0,4},{1,5},{2,6},{3,7},{4,0},{5,1},{6,2},{7,3},{8,12},{9,13},{10,... | collective-permute-start | bytes 98312 | tf_op jit(solution)/shard_map/ppermute | solution.py:396
  12.6 5.5 %collective-permute-start.32 = (f32[2,32,128]{2,1,0:T(8,128)}, f32[2,32,128]{2,1,0:T(8,128)S(1)}, u32[]{:S(2)}, u32[]{:S(2)}) collective-permute-start(f32[2,32,128]{2,1,0:T(8,128)} %refs_33_.1), channel_id=1, source_target_pairs={{0,2},{1,3},{2,0},{3,1},{4,6},{5,7},{6,4},{7,5},{8,10},{9,11},{10,... | collective-permute-start | bytes 98312 | tf_op jit(solution)/shard_map/ppermute | solution.py:396
  14.5 4.6 %collective-permute-start.31 = (f32[2,32,128]{2,1,0:T(8,128)}, f32[2,32,128]{2,1,0:T(8,128)S(1)}, u32[]{:S(2)}, u32[]{:S(2)}) collective-permute-start(f32[2,32,128]{2,1,0:T(8,128)} %refs_33_.1), channel_id=1, source_target_pairs={{0,1},{1,0},{2,3},{3,2},{4,5},{5,4},{6,7},{7,6},{8,9},{9,8},{10,11... | collective-permute-start | bytes 98312 | tf_op jit(solution)/shard_map/ppermute | solution.py:396
  16.0 4.2 %collective-permute-start.46 = (f32[2,32,128]{2,1,0:T(8,128)}, f32[2,32,128]{2,1,0:T(8,128)S(1)}, u32[]{:S(2)}, u32[]{:S(2)}) collective-permute-start(f32[2,32,128]{2,1,0:T(8,128)} %refs_33_.1), channel_id=1, source_target_pairs={{0,16},{8,24},{16,0},{24,8},{1,17},{9,25},{17,1},{25,9},{2,18},{10... | collective-permute-start | bytes 98312 | tf_op jit(solution)/shard_map/ppermute | solution.py:396
  17.5 3.9 %collective-permute-start.21 = (f32[2,32,128]{2,1,0:T(8,128)S(1)}, f32[2,32,128]{2,1,0:T(8,128)S(1)}, u32[]{:S(2)}, u32[]{:S(2)}) collective-permute-start(f32[2,32,128]{2,1,0:T(8,128)S(1)} %collective-permute-done.5.refs_7_), channel_id=1, source_target_pairs={{0,16},{8,24},{16,0},{24,8},{1,17},{9,25},{17,1},{25,9},{2,18},{10... | collective-permute-start | bytes 98312 | tf_op jit(solution)/shard_map/ppermute | solution.py:396
  18.0 3.9 %collective-permute-start.13 = (f32[2,32,128]{2,1,0:T(8,128)S(1)}, f32[2,32,128]{2,1,0:T(8,128)S(1)}, u32[]{:S(2)}, u32[]{:S(2)}) collective-permute-start(f32[2,32,128]{2,1,0:T(8,128)S(1)} %collective-permute-done.5.refs_7_), channel_id=1, source_target_pairs={{0,8},{8,0},{16,24},{24,16},{1,9},{9,1},{17,25},{25,17},{2,10},{10... | collective-permute-start | bytes 98312 | tf_op jit(solution)/shard_map/ppermute | solution.py:396
  18.0 4.9 %collective-permute-start.6 = (f32[2,32,128]{2,1,0:T(8,128)S(1)}, f32[2,32,128]{2,1,0:T(8,128)S(1)}, u32[]{:S(2)}, u32[]{:S(2)}) collective-permute-start(f32[2,32,128]{2,1,0:T(8,128)S(1)} %collective-permute-done.5.refs_7_), channel_id=1, source_target_pairs={{0,1},{1,0},{2,3},{3,2},{4,5},{5,4},{6,7},{7,6},{8,9},{9,8},{10,11... | collective-permute-start | bytes 98312 | tf_op jit(solution)/shard_map/ppermute | solution.py:396
  19.1 3.9 %collective-permute-start.19 = (f32[2,32,128]{2,1,0:T(8,128)S(1)}, f32[2,32,128]{2,1,0:T(8,128)S(1)}, u32[]{:S(2)}, u32[]{:S(2)}) collective-permute-start(f32[2,32,128]{2,1,0:T(8,128)S(1)} %collective-permute-done.3.refs_5_), channel_id=1, source_target_pairs={{0,16},{8,24},{16,0},{24,8},{1,17},{9,25},{17,1},{25,9},{2,18},{10... | collective-permute-start | bytes 98312 | tf_op jit(solution)/shard_map/ppermute | solution.py:396
  20.2 3.9 %collective-permute-start.11 = (f32[2,32,128]{2,1,0:T(8,128)S(1)}, f32[2,32,128]{2,1,0:T(8,128)S(1)}, u32[]{:S(2)}, u32[]{:S(2)}) collective-permute-start(f32[2,32,128]{2,1,0:T(8,128)S(1)} %collective-permute-done.3.refs_5_), channel_id=1, source_target_pairs={{0,8},{8,0},{16,24},{24,16},{1,9},{9,1},{17,25},{25,17},{2,10},{10... | collective-permute-start | bytes 98312 | tf_op jit(solution)/shard_map/ppermute | solution.py:396
  21.4 3.9 %collective-permute-start.4 = (f32[2,32,128]{2,1,0:T(8,128)S(1)}, f32[2,32,128]{2,1,0:T(8,128)S(1)}, u32[]{:S(2)}, u32[]{:S(2)}) collective-permute-start(f32[2,32,128]{2,1,0:T(8,128)S(1)} %collective-permute-done.3.refs_5_), channel_id=1, source_target_pairs={{0,1},{1,0},{2,3},{3,2},{4,5},{5,4},{6,7},{7,6},{8,9},{9,8},{10,11... | collective-permute-start | bytes 98312 | tf_op jit(solution)/shard_map/ppermute | solution.py:396
  22.0 3.9 %collective-permute-start.17 = (f32[2,32,128]{2,1,0:T(8,128)S(1)}, f32[2,32,128]{2,1,0:T(8,128)S(1)}, u32[]{:S(2)}, u32[]{:S(2)}) collective-permute-start(f32[2,32,128]{2,1,0:T(8,128)S(1)} %collective-permute-done.1.refs_3_), channel_id=1, source_target_pairs={{0,16},{8,24},{16,0},{24,8},{1,17},{9,25},{17,1},{25,9},{2,18},{10... | collective-permute-start | bytes 98312 | tf_op jit(solution)/shard_map/ppermute | solution.py:396
  23.0 4.4 %collective-permute-start.9 = (f32[2,32,128]{2,1,0:T(8,128)S(1)}, f32[2,32,128]{2,1,0:T(8,128)S(1)}, u32[]{:S(2)}, u32[]{:S(2)}) collective-permute-start(f32[2,32,128]{2,1,0:T(8,128)S(1)} %collective-permute-done.1.refs_3_), channel_id=1, source_target_pairs={{0,8},{8,0},{16,24},{24,16},{1,9},{9,1},{17,25},{25,17},{2,10},{10... | collective-permute-start | bytes 98312 | tf_op jit(solution)/shard_map/ppermute | solution.py:396
  23.0 4.9 %collective-permute-start.2 = (f32[2,32,128]{2,1,0:T(8,128)S(1)}, f32[2,32,128]{2,1,0:T(8,128)S(1)}, u32[]{:S(2)}, u32[]{:S(2)}) collective-permute-start(f32[2,32,128]{2,1,0:T(8,128)S(1)} %collective-permute-done.1.refs_3_), channel_id=1, source_target_pairs={{0,1},{1,0},{2,3},{3,2},{4,5},{5,4},{6,7},{7,6},{8,9},{9,8},{10,11... | collective-permute-start | bytes 98312 | tf_op jit(solution)/shard_map/ppermute | solution.py:396
  24.1 3.8 %collective-permute-start.8 = (f32[2,32,128]{2,1,0:T(8,128)S(1)}, f32[2,32,128]{2,1,0:T(8,128)S(1)}, u32[]{:S(2)}, u32[]{:S(2)}) collective-permute-start(f32[2,32,128]{2,1,0:T(8,128)S(1)} %collective-permute-done.refs_2_), channel_id=1, source_target_pairs={{0,8},{8,0},{16,24},{24,16},{1,9},{9,1},{17,25},{25,17},{2,10},{10... | collective-permute-start | bytes 98312 | tf_op jit(solution)/shard_map/ppermute | solution.py:396
  25.4 3.6 %collective-permute-start.23 = (f32[2,32,128]{2,1,0:T(8,128)S(1)}, f32[2,32,128]{2,1,0:T(8,128)S(1)}, u32[]{:S(2)}, u32[]{:S(2)}) collective-permute-start(f32[2,32,128]{2,1,0:T(8,128)S(1)} %collective-permute-done.15.refs_17_), channel_id=1, source_target_pairs={{0,8},{8,0},{16,24},{24,16},{1,9},{9,1},{17,25},{25,17},{2,10},{10... | collective-permute-start | bytes 98312 | tf_op jit(solution)/shard_map/ppermute | solution.py:396
  25.9 4.1 %collective-permute-start.16 = (f32[2,32,128]{2,1,0:T(8,128)S(1)}, f32[2,32,128]{2,1,0:T(8,128)S(1)}, u32[]{:S(2)}, u32[]{:S(2)}) collective-permute-start(f32[2,32,128]{2,1,0:T(8,128)S(1)} %collective-permute-done.15.refs_17_), channel_id=1, source_target_pairs={{0,1},{1,0},{2,3},{3,2},{4,5},{5,4},{6,7},{7,6},{8,9},{9,8},{10,11... | collective-permute-start | bytes 98312 | tf_op jit(solution)/shard_map/ppermute | solution.py:396
  27.4 3.9 %collective-permute-start.52 = (f32[2,32,128]{2,1,0:T(8,128)S(1)}, f32[2,32,128]{2,1,0:T(8,128)S(1)}, u32[]{:S(2)}, u32[]{:S(2)}) collective-permute-start(f32[2,32,128]{2,1,0:T(8,128)S(1)} %collective-permute-done.36.refs_39_), channel_id=1, source_target_pairs={{0,16},{8,24},{16,0},{24,8},{1,17},{9,25},{17,1},{25,9},{2,18},{10... | collective-permute-start | bytes 98312 | tf_op jit(solution)/shard_map/ppermute | solution.py:396
  28.0 3.9 %collective-permute-start.44 = (f32[2,32,128]{2,1,0:T(8,128)S(1)}, f32[2,32,128]{2,1,0:T(8,128)S(1)}, u32[]{:S(2)}, u32[]{:S(2)}) collective-permute-start(f32[2,32,128]{2,1,0:T(8,128)S(1)} %collective-permute-done.36.refs_39_), channel_id=1, source_target_pairs={{0,8},{8,0},{16,24},{24,16},{1,9},{9,1},{17,25},{25,17},{2,10},{10... | collective-permute-start | bytes 98312 | tf_op jit(solution)/shard_map/ppermute | solution.py:396
  28.0 4.9 %collective-permute-start.37 = (f32[2,32,128]{2,1,0:T(8,128)S(1)}, f32[2,32,128]{2,1,0:T(8,128)S(1)}, u32[]{:S(2)}, u32[]{:S(2)}) collective-permute-start(f32[2,32,128]{2,1,0:T(8,128)S(1)} %collective-permute-done.36.refs_39_), channel_id=1, source_target_pairs={{0,1},{1,0},{2,3},{3,2},{4,5},{5,4},{6,7},{7,6},{8,9},{9,8},{10,11... | collective-permute-start | bytes 98312 | tf_op jit(solution)/shard_map/ppermute | solution.py:396
  29.0 3.9 %collective-permute-start.50 = (f32[2,32,128]{2,1,0:T(8,128)S(1)}, f32[2,32,128]{2,1,0:T(8,128)S(1)}, u32[]{:S(2)}, u32[]{:S(2)}) collective-permute-start(f32[2,32,128]{2,1,0:T(8,128)S(1)} %collective-permute-done.34.refs_37_), channel_id=1, source_target_pairs={{0,16},{8,24},{16,0},{24,8},{1,17},{9,25},{17,1},{25,9},{2,18},{10... | collective-permute-start | bytes 98312 | tf_op jit(solution)/shard_map/ppermute | solution.py:396
  30.0 3.9 %collective-permute-start.42 = (f32[2,32,128]{2,1,0:T(8,128)S(1)}, f32[2,32,128]{2,1,0:T(8,128)S(1)}, u32[]{:S(2)}, u32[]{:S(2)}) collective-permute-start(f32[2,32,128]{2,1,0:T(8,128)S(1)} %collective-permute-done.34.refs_37_), channel_id=1, source_target_pairs={{0,8},{8,0},{16,24},{24,16},{1,9},{9,1},{17,25},{25,17},{2,10},{10... | collective-permute-start | bytes 98312 | tf_op jit(solution)/shard_map/ppermute | solution.py:396
  31.3 3.9 %collective-permute-start.35 = (f32[2,32,128]{2,1,0:T(8,128)S(1)}, f32[2,32,128]{2,1,0:T(8,128)S(1)}, u32[]{:S(2)}, u32[]{:S(2)}) collective-permute-start(f32[2,32,128]{2,1,0:T(8,128)S(1)} %collective-permute-done.34.refs_37_), channel_id=1, source_target_pairs={{0,1},{1,0},{2,3},{3,2},{4,5},{5,4},{6,7},{7,6},{8,9},{9,8},{10,11... | collective-permute-start | bytes 98312 | tf_op jit(solution)/shard_map/ppermute | solution.py:396
  31.8 3.9 %collective-permute-start.48 = (f32[2,32,128]{2,1,0:T(8,128)S(1)}, f32[2,32,128]{2,1,0:T(8,128)S(1)}, u32[]{:S(2)}, u32[]{:S(2)}) collective-permute-start(f32[2,32,128]{2,1,0:T(8,128)S(1)} %collective-permute-done.32.refs_35_), channel_id=1, source_target_pairs={{0,16},{8,24},{16,0},{24,8},{1,17},{9,25},{17,1},{25,9},{2,18},{10... | collective-permute-start | bytes 98312 | tf_op jit(solution)/shard_map/ppermute | solution.py:396
  32.8 4.4 %collective-permute-start.40 = (f32[2,32,128]{2,1,0:T(8,128)S(1)}, f32[2,32,128]{2,1,0:T(8,128)S(1)}, u32[]{:S(2)}, u32[]{:S(2)}) collective-permute-start(f32[2,32,128]{2,1,0:T(8,128)S(1)} %collective-permute-done.32.refs_35_), channel_id=1, source_target_pairs={{0,8},{8,0},{16,24},{24,16},{1,9},{9,1},{17,25},{25,17},{2,10},{10... | collective-permute-start | bytes 98312 | tf_op jit(solution)/shard_map/ppermute | solution.py:396
  32.9 4.4 %collective-permute-start.33 = (f32[2,32,128]{2,1,0:T(8,128)S(1)}, f32[2,32,128]{2,1,0:T(8,128)S(1)}, u32[]{:S(2)}, u32[]{:S(2)}) collective-permute-start(f32[2,32,128]{2,1,0:T(8,128)S(1)} %collective-permute-done.32.refs_35_), channel_id=1, source_target_pairs={{0,1},{1,0},{2,3},{3,2},{4,5},{5,4},{6,7},{7,6},{8,9},{9,8},{10,11... | collective-permute-start | bytes 98312 | tf_op jit(solution)/shard_map/ppermute | solution.py:396
  34.0 3.9 %collective-permute-start.39 = (f32[2,32,128]{2,1,0:T(8,128)S(1)}, f32[2,32,128]{2,1,0:T(8,128)S(1)}, u32[]{:S(2)}, u32[]{:S(2)}) collective-permute-start(f32[2,32,128]{2,1,0:T(8,128)S(1)} %collective-permute-done.31.refs_34_), channel_id=1, source_target_pairs={{0,8},{8,0},{16,24},{24,16},{1,9},{9,1},{17,25},{25,17},{2,10},{10... | collective-permute-start | bytes 98312 | tf_op jit(solution)/shard_map/ppermute | solution.py:396
  35.8 3.9 %collective-permute-start.47 = (f32[2,32,128]{2,1,0:T(8,128)S(1)}, f32[2,32,128]{2,1,0:T(8,128)S(1)}, u32[]{:S(2)}, u32[]{:S(2)}) collective-permute-start(f32[2,32,128]{2,1,0:T(8,128)S(1)} %collective-permute-done.46.refs_49_), channel_id=1, source_target_pairs={{0,1},{1,0},{2,3},{3,2},{4,5},{5,4},{6,7},{7,6},{8,9},{9,8},{10,11... | collective-permute-start | bytes 98312 | tf_op jit(solution)/shard_map/ppermute | solution.py:396
  37.3 4.2 %collective-permute-start.29 = (f32[2,32,128]{2,1,0:T(8,128)S(1)}, f32[2,32,128]{2,1,0:T(8,128)S(1)}, u32[]{:S(2)}, u32[]{:S(2)}) collective-permute-start(f32[2,32,128]{2,1,0:T(8,128)S(1)} %collective-permute-done.21.refs_23_), channel_id=1, source_target_pairs={{0,8},{8,0},{16,24},{24,16},{1,9},{9,1},{17,25},{25,17},{2,10},{10... | collective-permute-start | bytes 98312 | tf_op jit(solution)/shard_map/ppermute | solution.py:396
  37.3 4.2 %collective-permute-start.22 = (f32[2,32,128]{2,1,0:T(8,128)S(1)}, f32[2,32,128]{2,1,0:T(8,128)S(1)}, u32[]{:S(2)}, u32[]{:S(2)}) collective-permute-start(f32[2,32,128]{2,1,0:T(8,128)S(1)} %collective-permute-done.21.refs_23_), channel_id=1, source_target_pairs={{0,1},{1,0},{2,3},{3,2},{4,5},{5,4},{6,7},{7,6},{8,9},{9,8},{10,11... | collective-permute-start | bytes 98312 | tf_op jit(solution)/shard_map/ppermute | solution.py:396
  37.9 4.1 %collective-permute-start.14 = (f32[2,32,128]{2,1,0:T(8,128)S(1)}, f32[2,32,128]{2,1,0:T(8,128)S(1)}, u32[]{:S(2)}, u32[]{:S(2)}) collective-permute-start(f32[2,32,128]{2,1,0:T(8,128)S(1)} %collective-permute-done.6.refs_8_), channel_id=1, source_target_pairs={{0,8},{8,0},{16,24},{24,16},{1,9},{9,1},{17,25},{25,17},{2,10},{10... | collective-permute-start | bytes 98312 | tf_op jit(solution)/shard_map/ppermute | solution.py:396
  38.0 4.2 %collective-permute-start.27 = (f32[2,32,128]{2,1,0:T(8,128)S(1)}, f32[2,32,128]{2,1,0:T(8,128)S(1)}, u32[]{:S(2)}, u32[]{:S(2)}) collective-permute-start(f32[2,32,128]{2,1,0:T(8,128)S(1)} %collective-permute-done.19.refs_21_), channel_id=1, source_target_pairs={{0,8},{8,0},{16,24},{24,16},{1,9},{9,1},{17,25},{25,17},{2,10},{10... | collective-permute-start | bytes 98312 | tf_op jit(solution)/shard_map/ppermute | solution.py:396
  39.7 3.9 %collective-permute-start.20 = (f32[2,32,128]{2,1,0:T(8,128)S(1)}, f32[2,32,128]{2,1,0:T(8,128)S(1)}, u32[]{:S(2)}, u32[]{:S(2)}) collective-permute-start(f32[2,32,128]{2,1,0:T(8,128)S(1)} %collective-permute-done.19.refs_21_), channel_id=1, source_target_pairs={{0,1},{1,0},{2,3},{3,2},{4,5},{5,4},{6,7},{7,6},{8,9},{9,8},{10,11... | collective-permute-start | bytes 98312 | tf_op jit(solution)/shard_map/ppermute | solution.py:396
  42.0 4.2 %collective-permute-start.18 = (f32[2,32,128]{2,1,0:T(8,128)S(1)}, f32[2,32,128]{2,1,0:T(8,128)S(1)}, u32[]{:S(2)}, u32[]{:S(2)}) collective-permute-start(f32[2,32,128]{2,1,0:T(8,128)S(1)} %collective-permute-done.17.refs_19_), channel_id=1, source_target_pairs={{0,1},{1,0},{2,3},{3,2},{4,5},{5,4},{6,7},{7,6},{8,9},{9,8},{10,11... | collective-permute-start | bytes 98312 | tf_op jit(solution)/shard_map/ppermute | solution.py:396
  42.2 4.0 %collective-permute-start.10 = (f32[2,32,128]{2,1,0:T(8,128)S(1)}, f32[2,32,128]{2,1,0:T(8,128)S(1)}, u32[]{:S(2)}, u32[]{:S(2)}) collective-permute-start(f32[2,32,128]{2,1,0:T(8,128)S(1)} %collective-permute-done.2.refs_4_), channel_id=1, source_target_pairs={{0,8},{8,0},{16,24},{24,16},{1,9},{9,1},{17,25},{25,17},{2,10},{10... | collective-permute-start | bytes 98312 | tf_op jit(solution)/shard_map/ppermute | solution.py:396
  43.6 3.3 %collective-permute-start.60 = (f32[2,32,128]{2,1,0:T(8,128)S(1)}, f32[2,32,128]{2,1,0:T(8,128)S(1)}, u32[]{:S(2)}, u32[]{:S(2)}) collective-permute-start(f32[2,32,128]{2,1,0:T(8,128)S(1)} %collective-permute-done.52.refs_55_), channel_id=1, source_target_pairs={{0,8},{8,0},{16,24},{24,16},{1,9},{9,1},{17,25},{25,17},{2,10},{10... | collective-permute-start | bytes 98312 | tf_op jit(solution)/shard_map/ppermute | solution.py:396
  44.1 4.0 %collective-permute-start.53 = (f32[2,32,128]{2,1,0:T(8,128)S(1)}, f32[2,32,128]{2,1,0:T(8,128)S(1)}, u32[]{:S(2)}, u32[]{:S(2)}) collective-permute-start(f32[2,32,128]{2,1,0:T(8,128)S(1)} %collective-permute-done.52.refs_55_), channel_id=1, source_target_pairs={{0,1},{1,0},{2,3},{3,2},{4,5},{5,4},{6,7},{7,6},{8,9},{9,8},{10,11... | collective-permute-start | bytes 98312 | tf_op jit(solution)/shard_map/ppermute | solution.py:396
  46.2 4.2 %collective-permute-start.58 = (f32[2,32,128]{2,1,0:T(8,128)S(1)}, f32[2,32,128]{2,1,0:T(8,128)S(1)}, u32[]{:S(2)}, u32[]{:S(2)}) collective-permute-start(f32[2,32,128]{2,1,0:T(8,128)S(1)} %collective-permute-done.50.refs_53_), channel_id=1, source_target_pairs={{0,8},{8,0},{16,24},{24,16},{1,9},{9,1},{17,25},{25,17},{2,10},{10... | collective-permute-start | bytes 98312 | tf_op jit(solution)/shard_map/ppermute | solution.py:396
  46.7 3.9 %collective-permute-start.51 = (f32[2,32,128]{2,1,0:T(8,128)S(1)}, f32[2,32,128]{2,1,0:T(8,128)S(1)}, u32[]{:S(2)}, u32[]{:S(2)}) collective-permute-start(f32[2,32,128]{2,1,0:T(8,128)S(1)} %collective-permute-done.50.refs_53_), channel_id=1, source_target_pairs={{0,1},{1,0},{2,3},{3,2},{4,5},{5,4},{6,7},{7,6},{8,9},{9,8},{10,11... | collective-permute-start | bytes 98312 | tf_op jit(solution)/shard_map/ppermute | solution.py:396
  46.9 4.0 %collective-permute-start.43 = (f32[2,32,128]{2,1,0:T(8,128)S(1)}, f32[2,32,128]{2,1,0:T(8,128)S(1)}, u32[]{:S(2)}, u32[]{:S(2)}) collective-permute-start(f32[2,32,128]{2,1,0:T(8,128)S(1)} %collective-permute-done.35.refs_38_), channel_id=1, source_target_pairs={{0,8},{8,0},{16,24},{24,16},{1,9},{9,1},{17,25},{25,17},{2,10},{10... | collective-permute-start | bytes 98312 | tf_op jit(solution)/shard_map/ppermute | solution.py:396
  48.1 4.3 %collective-permute-start.49 = (f32[2,32,128]{2,1,0:T(8,128)S(1)}, f32[2,32,128]{2,1,0:T(8,128)S(1)}, u32[]{:S(2)}, u32[]{:S(2)}) collective-permute-start(f32[2,32,128]{2,1,0:T(8,128)S(1)} %collective-permute-done.48.refs_51_), channel_id=1, source_target_pairs={{0,1},{1,0},{2,3},{3,2},{4,5},{5,4},{6,7},{7,6},{8,9},{9,8},{10,11... | collective-permute-start | bytes 98312 | tf_op jit(solution)/shard_map/ppermute | solution.py:396
  (17 other events, 31.8 us)

commit v2 on v1

--- a/solution.py
+++ b/solution.py
@@ -36,28 +36,38 @@
         self.count = self.pages * planes
 
     def shape(self):
-        return (self.count * self.height, LANES)
+        return ((self.count + 2 * self.planes) * self.height, LANES)
 
     def base(self, strip, tile):
-        return pl.multiple_of(SUB + strip * self.pitch + tile * SUB, SUB)
+        row = SUB + strip * self.pitch + tile * SUB
+        return row if isinstance(row, int) else pl.multiple_of(row, SUB)
+
+    def at(self, page, plane, row):
+        return ((page + 1) * self.planes + plane) * self.height + row
 
 
 def tile_of(ref, level, page, plane, row):
-    return ref[pl.ds((page * level.planes + plane) * level.height + row, SUB), :]
+    return ref[pl.ds(level.at(page, plane, row), SUB), :]
 
 
 def put_tile(ref, level, page, plane, row, value):
-    ref[pl.ds((page * level.planes + plane) * level.height + row, SUB), :] = value
+    ref[pl.ds(level.at(page, plane, row), SUB), :] = value
 
 
 def fill_halo(ref, level, offsets, step, halo):
     count, width = level.count, level.pages
+    for strip in range(level.strips):
+        for tile in range(level.tiles):
+            for z in range(level.planes):
+                row = level.base(strip, tile)
+                put_tile(ref, level, width, z, row, pltpu.roll(tile_of(ref, level, 0, z, row), LANES - 1, 1))
+                put_tile(ref, level, -1, z, row, pltpu.roll(tile_of(ref, level, width - 1, z, row), 1, 1))
     for strip in range(level.strips):
         shift = offsets[step, strip] // level.factor
         lane, page = shift // width, shift % width
         under = (strip - 1) % level.strips
-        first = SUB + strip * level.pitch
-        last = SUB + under * level.pitch + level.rows - 1
+        first = level.at(0, 0, SUB + strip * level.pitch)
+        last = level.at(0, 0, SUB) + under * level.pitch + level.rows - 1
         upper = ref[pl.ds(first, count, stride=level.height), :]
         lower = ref[pl.ds(last, count, stride=level.height), :]
         start = strip * 4 * count
@@ -71,20 +81,30 @@
         ]
 
 
+UNROLLED = 8
+
+
+def repeat(count, body, carry):
+    if count > UNROLLED:
+        return lax.fori_loop(0, count, body, carry)
+    for index in range(count):
+        carry = body(index, carry)
+    return carry
+
+
 def stencil(ref, level, base):
     planes, width = level.planes, level.pages
-    cell = [[tile_of(ref, level, p, z, base) for z in range(planes)] for p in range(width)]
+    cell = [[tile_of(ref, level, p, z, base) for z in range(planes)] for p in range(-1, width + 1)]
     out = []
     for p in range(width):
         row = []
         for z in range(planes):
-            right = cell[p + 1][z] if p + 1 < width else pltpu.roll(cell[0][z], LANES - 1, 1)
-            left = cell[p - 1][z] if p else pltpu.roll(cell[width - 1][z], 1, 1)
+            left, here, right = cell[p][z], cell[p + 1][z], cell[p + 2][z]
             above = tile_of(ref, level, p, z, base + 1)
             below = tile_of(ref, level, p, z, base - 1)
             beside = (above + below) + (right + left)
-            vertical = cell[p][(z + 1) % planes] + cell[p][(z - 1) % planes]
-            row.append((cell[p][z], right, left, beside, vertical))
+            vertical = cell[p + 1][(z + 1) % planes] + cell[p + 1][(z - 1) % planes]
+            row.append((here, right, left, beside, vertical))
         out.append(row)
     return out
 
@@ -98,11 +118,21 @@
     return level.diagonal * cell - level.coupling * beside - VERTICAL * vertical
 
 
+def loop_coarse(coarse, body):
+    count = coarse.strips * coarse.tiles
+    if coarse.factor > 2:
+        for index in range(count):
+            body(index, 0)
+    else:
+        lax.fori_loop(0, count, body, 0)
+
+
 def restrict(ref, level, coarse_ref, coarse, pairs):
     planes = level.planes
 
     def body(index, carry):
         strip, tile = index // coarse.tiles, index % coarse.tiles
+        room = index * coarse.count * 2 * SUB if isinstance(index, int) else 0
         for half in range(2):
             base = level.base(strip, 2 * tile + half)
             terms = stencil(ref, level, base)
@@ -112,16 +142,16 @@
                     for q in (2 * p, 2 * p + 1):
                         cell, _, _, beside, vertical = terms[q][z]
                         total = total + smooth(level, cell, beside, vertical)
-                    pairs[pl.ds((p * planes + z) * 2 * SUB + half * SUB, SUB), :] = total
+                    pairs[pl.ds(room + (p * planes + z) * 2 * SUB + half * SUB, SUB), :] = total
         for p in range(coarse.pages):
             for z in range(planes):
-                start = (p * planes + z) * 2 * SUB
+                start = room + (p * planes + z) * 2 * SUB
                 even = pairs[pl.ds(start, SUB, stride=2), :]
                 odd = pairs[pl.ds(start + 1, SUB, stride=2), :]
                 put_tile(coarse_ref, coarse, p, z, coarse.base(strip, tile), 0.25 * (even + odd))
         return carry
 
-    lax.fori_loop(0, coarse.strips * coarse.tiles, body, 0)
+    loop_coarse(coarse, body)
 
 
 def prolong(coarse_ref, coarse, residual, level, ref, pairs):
@@ -129,15 +159,16 @@
 
     def body(index, carry):
         strip, tile = index // coarse.tiles, index % coarse.tiles
+        room = index * coarse.count * 2 * SUB if isinstance(index, int) else 0
         for p in range(coarse.pages):
             for z in range(planes):
-                start = (p * planes + z) * 2 * SUB
+                start = room + (p * planes + z) * 2 * SUB
                 value = tile_of(coarse_ref, coarse, p, z, coarse.base(strip, tile))
                 pairs[pl.ds(start, SUB, stride=2), :] = value
                 pairs[pl.ds(start + 1, SUB, stride=2), :] = value
         for p in range(coarse.pages):
             for z in range(planes):
-                start = (p * planes + z) * 2 * SUB
+                start = room + (p * planes + z) * 2 * SUB
                 for half in range(2):
                     value = pairs[pl.ds(start + half * SUB, SUB), :]
                     base = level.base(strip, 2 * tile + half)
@@ -145,7 +176,7 @@
                         put_tile(ref, level, q, z, base, level.relax * tile_of(residual, level, q, z, base) + value)
         return carry
 
-    lax.fori_loop(0, coarse.strips * coarse.tiles, body, 0)
+    loop_coarse(coarse, body)
 
 
 def per_tile(level, body, sums):
@@ -153,7 +184,7 @@
         return body(level.base(index // level.tiles, index % level.tiles), carry)
 
     zero = jnp.zeros((SUB, LANES), jnp.float32)
-    return lax.fori_loop(0, level.strips * level.tiles, step, (zero,) * sums)
+    return repeat(level.strips * level.tiles, step, (zero,) * sums)
 
 
 def total(vector):
@@ -203,30 +234,38 @@
     fill_halo(estimate, level, offsets, step, halo)
 
 
-def interleave(ref, level):
+def interleave(blocks, dy_count, level, gy, gx, targets, stage):
     width, planes = level.pages, level.planes
     lane = lax.broadcasted_iota(jnp.int32, (SUB, LANES), 1)
     per = LANES // width
     source = (lane % per) * width + lane // per
-
-    def body(index, carry):
-        base = level.base(index // level.tiles, index % level.tiles)
-        for z in range(planes):
-            pages = [tile_of(ref, level, p, z, base) for p in range(width)]
-            bit = 1
-            while bit < width:
-                low = (lane // bit) % 2 == 0
-                for p in range(width):
-                    if not p & bit:
-                        a, b = pages[p], pages[p | bit]
-                        pages[p] = jnp.where(low, a, pltpu.roll(b, bit, 1))
-                        pages[p | bit] = jnp.where(low, pltpu.roll(a, LANES - bit, 1), b)
-                bit *= 2
+    groups = [
+        (name, dy, z, tile) for name in range(len(targets)) for dy in range(dy_count) for z in range(planes) for tile in range(level.tiles)
+    ]
+
+    def slot(turn, group, page):
+        return pl.ds(((turn % 2 * len(groups) + group) * width + page) * SUB, SUB)
+
+    bits = [1 << i for i in range(width.bit_length() - 1)]
+    for turn, bit in enumerate(bits):
+        mine = (gx // bit) % 2
+        keep = (lane // bit + mine) % 2 == 0
+        shift = jnp.where(mine == 0, bit, LANES - bit)
+        for group, (name, dy, z, tile) in enumerate(groups):
             for p in range(width):
-                put_tile(ref, level, p, z, base, jnp.take_along_axis(pages[p], source, axis=1))
-        return carry
-
-    lax.fori_loop(0, level.strips * level.tiles, body, 0)
+                if p & bit:
+                    continue
+                if turn == 0:
+                    a, b = (blocks(name, dy, q, z, tile) for q in (p, p | bit))
+                else:
+                    a, b = (stage[slot(turn, group, q), :] for q in (p, p | bit))
+                stage[slot(turn + 1, group, p), :] = jnp.where(keep, a, pltpu.roll(b, shift, 1))
+                stage[slot(turn + 1, group, p | bit), :] = jnp.where(keep, pltpu.roll(a, LANES - shift, 1), b)
+    for group, (name, dy, z, tile) in enumerate(groups):
+        row = level.base(jnp.bitwise_xor(gy, dy), tile)
+        for p in range(width):
+            value = jnp.take_along_axis(stage[slot(len(bits), group, p), :], source, axis=1)
+            put_tile(targets[name], level, jnp.bitwise_xor(gx, p), z, row, value)
 
 
 def solve(offsets, u, v, r, q, w, work, halo, pairs, levels):
@@ -327,29 +366,17 @@
     return update
 
 
-def whole_kernel(keys, levels, *refs):
-    count = len(keys)
-    offsets, blocks, out = refs[0], refs[1 : 1 + count], refs[1 + count]
-    u, v, r, q, w, e, r1, e1, f1, r2, e2, f2, halo, pairs, sems = refs[2 + count :]
+def whole_kernel(places, arrays, levels, *refs):
+    offsets, held, out = refs[0], refs[1 : 1 + arrays], refs[1 + arrays]
+    u, v, r, q, w, e, r1, e1, f1, r2, e2, f2, halo, pairs, stage = refs[2 + arrays :]
     fine = levels[0]
     gy, gx = lax.axis_index("gy"), lax.axis_index("gx")
-    copies = []
-    for index, (name, dy, dx) in enumerate(keys):
-        target = u if name == "u" else v
-        row = SUB + jnp.bitwise_xor(gy, dy) * fine.pitch
-        for z in range(fine.planes):
-            start = (jnp.bitwise_xor(gx, dx) * fine.planes + z) * fine.height + row
-            copy = pltpu.make_async_copy(
-                blocks[index].at[z],
-                target.at[pl.ds(pl.multiple_of(start, SUB), fine.rows), :],
-                sems.at[index * fine.planes + z],
-            )
-            copy.start()
-            copies.append(copy)
-    for copy in copies:
-        copy.wait()
-    interleave(u, fine)
-    interleave(v, fine)
+
+    def block(name, dy, dx, z, tile):
+        array, place = places[dy, dx]
+        return held[array][place, name, z, pl.ds(tile * SUB, SUB), :]
+
+    interleave(block, fine.strips, fine, gy, gx, (u, v), stage)
     work = [[r, e], [r1, e1, f1], [r2, e2, f2]]
     update = solve(offsets, u, v, r, q, w, work, halo, pairs, levels)
     lane = lax.broadcasted_iota(jnp.int32, (SUB, LANES), 1)
@@ -365,30 +392,29 @@
             out[z, pl.ds(tile * SUB, SUB), :] = value
 
 
-def on_whole(blocks, offsets, strips, width):
-    keys = sorted(blocks)
-    planes, rows, columns = blocks[keys[0]].shape
+def on_whole(arrays, places, offsets, strips, width):
+    _, _, planes, rows, columns = arrays[0].shape
     levels = [Level(i, width, rows, strips, planes) for i in range(LEVELS)]
     fields = [pltpu.VMEM(levels[0].shape(), jnp.float32)] * 6
     fields += [pltpu.VMEM(levels[1].shape(), jnp.float32)] * 3 + [pltpu.VMEM(levels[2].shape(), jnp.float32)] * 3
     count = levels[0].count
     scratch = fields + [
         pltpu.VMEM((strips * 4 * count, LANES), jnp.float32),
-        pltpu.VMEM((count * SUB, LANES), jnp.float32),
-        pltpu.SemaphoreType.DMA((len(keys) * planes,)),
+        pltpu.VMEM((count * SUB * 2, LANES), jnp.float32),
+        pltpu.VMEM((2 * 2 * planes * strips * rows * width, LANES), jnp.float32),
     ]
 
     def kernel(*refs):
-        whole_kernel(keys, levels, *refs)
+        whole_kernel(places, len(arrays), levels, *refs)
 
     return pl.pallas_call(
         kernel,
         out_shape=jax.ShapeDtypeStruct((planes, rows, columns), jnp.float32),
-        in_specs=[pl.BlockSpec(memory_space=pltpu.SMEM)] + [pl.BlockSpec(memory_space=pl.ANY)] * len(keys),
+        in_specs=[pl.BlockSpec(memory_space=pltpu.SMEM)] + [pl.BlockSpec(memory_space=pltpu.VMEM)] * len(arrays),
         out_specs=pl.BlockSpec(memory_space=pltpu.VMEM),
         scratch_shapes=scratch,
         compiler_params=pltpu.CompilerParams(vmem_limit_bytes=48 << 20),
-    )(offsets, *[blocks[key] for key in keys])
+    )(offsets, *arrays)
 
 
 def swapped(block, axis, bits):
@@ -397,18 +423,27 @@
 
 
 def gathered(phase, velocity):
-    out = {}
-    for name, own in (("u", phase), ("v", velocity)):
-        out[name, 0, 0] = own
-        for k in (2, 4, 6):
-            out[name, 0, k] = swapped(own, "gx", k)
-        for k in (0, 2, 4, 6):
-            out[name, 0, k | 1] = swapped(out[name, 0, k], "gx", 1)
-            out[name, 2, k] = swapped(out[name, 0, k], "gy", 2)
-            out[name, 2, k | 1] = swapped(out[name, 2, k], "gx", 1)
-    for (name, dy, dx), block in list(out.items()):
-        out[name, dy ^ 1, dx] = swapped(block, "gy", 1)
-    return out
+    width = lax.axis_size("gx")
+    own = jnp.stack([phase, velocity])[None]
+    steps = list(range(0, width, 2))
+    half = len(steps) // 2
+    line = jnp.concatenate([own] + [swapped(own, "gx", k) for k in steps[1:]])
+    across = swapped(line, "gx", 1)
+    along = swapped(line, "gy", 2)
+    corner = [swapped(across[:half], "gy", 2), swapped(along[half:], "gx", 1)]
+    arrays = [line, across, along] + corner
+    arrays += [swapped(array, "gy", 1) for array in arrays]
+    places = {}
+    for core in range(2):
+        for i, k in enumerate(steps):
+            for dy, dx, array, place in (
+                (0, 0, 0, i),
+                (0, 1, 1, i),
+                (2, 0, 2, i),
+                (2, 1, 3 if i < half else 4, i % half),
+            ):
+                places[dy ^ core, dx ^ k] = (array + 5 * core, place)
+    return arrays, places
 
 
 def padded(cells, sides, width):
@@ -544,10 +579,10 @@
     strips, width = lax.axis_size("gy"), lax.axis_size("gx")
     planes, rows, columns = phase.shape
     sizes = Level(0, width, rows, strips, planes).shape()
-    fits = 8 * 4 * sizes[0] * sizes[1] < MOST_BYTES and strips * width <= MOST_DEVICES
-    shaped = columns == LANES and rows % 32 == 0 and width in (8, 16, 32, 64) and strips % 4 == 0
+    fits = 10 * 4 * sizes[0] * sizes[1] < MOST_BYTES and strips * width <= MOST_DEVICES
+    shaped = columns == LANES and rows % 32 == 0 and width in (8, 16, 32, 64) and strips == 4
     if fits and shaped:
-        return on_whole(gathered(phase, velocity), offsets, strips, width)
+        return on_whole(*gathered(phase, velocity), offsets, strips, width)
     return spread(phase, velocity, offsets)
 
 

time: 104 us -> 48.2 us (0.46)
  starting transfers between devices: 41.3 us -> 12.6 us
  Pallas kernels: 46.9 us -> 19.5 us
  local copies, waits for them, and re-layouts: 2.19 us -> 0.03 us
  waiting for transfers between devices: 13 us -> 15.1 us
    ppermute x62 -> x12, starting transfers between devices: 41.3 us -> 12.6 us  [swapped(): return lax.ppermute(block, axis, [(i, i ^ bits) for i in range(count)])]
    pallas_call x1, Pallas kernels: 46.9 us -> 19.5 us  [on_whole(): pl.pallas_call(kernel, out_shape=jax.ShapeDtypeStruct((planes, rows, colu...]
    unnamed x6 -> x2, local copies, waits for them, and re-layouts: 2.19 us -> 0.01 us
    ppermute x62 -> x12, waiting for transfers between devices: 13 us -> 15.1 us  [swapped(): return lax.ppermute(block, axis, [(i, i ^ bits) for i in range(count)])]
  transfers between devices with their start and end apart: 62 -> 12, of which waited for: 17 -> 6; matrix products, arithmetic and copies ran while one was open for 0% -> 0% of each run, Pallas kernels for 0% -> 0%
where the time goes in v2:
time: 48.2 us; the launch traced here: 48 us
  Pallas kernels  19.5 us (40%)
  waiting for transfers between devices  15.1 us (31%)
  starting transfers between devices  12.6 us (26%)
  other arithmetic  0.8 us (2%)
    pallas_call x1, Pallas kernels, on_whole(): pl.pallas_call(kernel, out_shape=jax.ShapeDtypeStruct((planes, rows, colu...  19.5 us
    ppermute x12, waiting for transfers between devices, swapped(): return lax.ppermute(block, axis, [(i, i ^ bits) for i in range(count)])  15.1 us
    ppermute x12, starting transfers between devices, swapped(): return lax.ppermute(block, axis, [(i, i ^ bits) for i in range(count)])  12.6 us
  transfers between devices with their start and end apart: 12, of which 6 were waited for; matrix products, arithmetic and copies ran while one was open for 0% of the time, Pallas kernels for 0%

profile of v2, /device:TPU:0, one launch (start us, length us, event | category | flops | bytes accessed | tf_op | source)
XLA Modules:
  0.0 48.0 jit_solution(15016110903967137644)
XLA Ops:
  0.0 0.8 %maximum_bitcast_fusion = f32[1,2,2,32,128]{4,3,2,1,0:T(8,128)S(1)} fusion(f32[1,2,32,128]{3,2,1,0:T(8,128)} %bitcast.4, f32[1,2,32,128]{3,2,1,0:T(8,128)} %bitcast.5), kind=kLoop, calls=%fused_computation.1 | loop fusion | flops 16384 | bytes 131072 | tf_op jit(solution)/shard_map/broadcast_in_dim | solution.py:427
  0.8 5.1 %collective-permute-start.2 = (f32[1,2,2,32,128]{4,3,2,1,0:T(8,128)S(1)}, f32[1,2,2,32,128]{4,3,2,1,0:T(8,128)S(1)}, u32[]{:S(2)}, u32[]{:S(2)}) collective-permute-start(f32[1,2,2,32,128]{4,3,2,1,0:T(8,128)S(1)} %maximum_bitcast_fusion), channel_id=1, source_target_pairs={{0,6},{1,7},{2,4},{3,5},{4,2},{5,3},{6,0},{7,1},{8,14},{9,15},{10,... | collective-permute-start | bytes 196616 | tf_op jit(solution)/shard_map/ppermute | solution.py:422
  5.9 0.0 collective-permute-start.1
  5.9 0.6 %collective-permute-start = (f32[1,2,2,32,128]{4,3,2,1,0:T(8,128)S(1)}, f32[1,2,2,32,128]{4,3,2,1,0:T(8,128)S(1)}, u32[]{:S(2)}, u32[]{:S(2)}) collective-permute-start(f32[1,2,2,32,128]{4,3,2,1,0:T(8,128)S(1)} %maximum_bitcast_fusion), channel_id=1, source_target_pairs={{0,2},{1,3},{2,0},{3,1},{4,6},{5,7},{6,4},{7,5},{8,10},{9,11},{10,... | collective-permute-start | bytes 196616 | tf_op jit(solution)/shard_map/ppermute | solution.py:422
  6.5 1.8 %collective-permute-done.2 = f32[1,2,2,32,128]{4,3,2,1,0:T(8,128)S(1)} collective-permute-done((f32[1,2,2,32,128]{4,3,2,1,0:T(8,128)S(1)}, f32[1,2,2,32,128]{4,3,2,1,0:T(8,128)S(1)}, u32[]{:S(2)}, u32[]{:S(2)}) %collective-permute-start.2) | collective-permute-done | bytes 65568 | tf_op jit(solution)/shard_map/ppermute | solution.py:422
  8.3 3.1 %collective-permute-done.1 = f32[1,2,2,32,128]{4,3,2,1,0:T(8,128)S(1)} collective-permute-done((f32[1,2,2,32,128]{4,3,2,1,0:T(8,128)S(1)}, f32[1,2,2,32,128]{4,3,2,1,0:T(8,128)S(1)}, u32[]{:S(2)}, u32[]{:S(2)}) %collective-permute-start.1) | collective-permute-done | bytes 65568 | tf_op jit(solution)/shard_map/ppermute | solution.py:422
  11.5 0.0 collective-permute-done
  11.5 1.6 %collective-permute-start.4 = (f32[4,2,2,32,128]{4,3,2,1,0:T(8,128)S(1)}, f32[4,2,2,32,128]{4,3,2,1,0:T(8,128)S(1)}, u32[]{:S(2)}, u32[]{:S(2)}) collective-permute-start(f32[4,2,2,32,128]{4,3,2,1,0:T(8,128)S(1)} %pad_maximum_fusion.refs_1_), channel_id=1, source_target_pairs={{0,16},{8,24},{16,0},{24,8},{1,17},{9,25},{17,1},{25,9},{2,18},{10... | collective-permute-start | bytes 786440 | tf_op jit(solution)/shard_map/ppermute | solution.py:422
  13.1 1.5 %collective-permute-start.3 = (f32[4,2,2,32,128]{4,3,2,1,0:T(8,128)S(1)}, f32[4,2,2,32,128]{4,3,2,1,0:T(8,128)S(1)}, u32[]{:S(2)}, u32[]{:S(2)}) collective-permute-start(f32[4,2,2,32,128]{4,3,2,1,0:T(8,128)S(1)} %pad_maximum_fusion.refs_1_), channel_id=1, source_target_pairs={{0,1},{1,0},{2,3},{3,2},{4,5},{5,4},{6,7},{7,6},{8,9},{9,8},{10,11... | collective-permute-start | bytes 786440 | tf_op jit(solution)/shard_map/ppermute | solution.py:422
  14.6 0.0 collective-permute-start.7
  14.6 4.9 %collective-permute-done.4.refs_3_ = f32[4,2,2,32,128]{4,3,2,1,0:T(8,128)S(1)} collective-permute-done((f32[4,2,2,32,128]{4,3,2,1,0:T(8,128)S(1)}, f32[4,2,2,32,128]{4,3,2,1,0:T(8,128)S(1)}, u32[]{:S(2)}, u32[]{:S(2)}) %collective-permute-start.4) | collective-permute-done | bytes 262176 | tf_op jit(solution)/shard_map/ppermute | solution.py:422
  19.4 0.0 copy-start
  19.5 1.7 %collective-permute-start.6 = (f32[2,2,2,32,128]{4,3,2,1,0:T(8,128)S(1)}, f32[2,2,2,32,128]{4,3,2,1,0:T(8,128)S(1)}, u32[]{:S(2)}, u32[]{:S(2)}) collective-permute-start(f32[2,2,2,32,128]{4,3,2,1,0:T(8,128)S(1)} %slice.9), channel_id=1, source_target_pairs={{0,1},{1,0},{2,3},{3,2},{4,5},{5,4},{6,7},{7,6},{8,9},{9,8},{10,11... | collective-permute-start | bytes 393224 | tf_op jit(solution)/shard_map/ppermute | solution.py:422
  21.1 0.0 collective-permute-start.9
  21.1 0.0 collective-permute-done.3.refs_2_
  21.1 0.6 %collective-permute-start.8 = (f32[4,2,2,32,128]{4,3,2,1,0:T(8,128)S(1)}, f32[4,2,2,32,128]{4,3,2,1,0:T(8,128)S(1)}, u32[]{:S(2)}, u32[]{:S(2)}) collective-permute-start(f32[4,2,2,32,128]{4,3,2,1,0:T(8,128)S(1)} %collective-permute-done.3.refs_2_), channel_id=1, source_target_pairs={{0,8},{8,0},{16,24},{24,16},{1,9},{9,1},{17,25},{25,17},{2,10},{10... | collective-permute-start | bytes 786440 | tf_op jit(solution)/shard_map/ppermute | solution.py:422
  21.7 1.5 %collective-permute-start.5 = (f32[2,2,2,32,128]{4,3,2,1,0:T(8,128)S(1)}, f32[2,2,2,32,128]{4,3,2,1,0:T(8,128)S(1)}, u32[]{:S(2)}, u32[]{:S(2)}) collective-permute-start(f32[2,2,2,32,128]{4,3,2,1,0:T(8,128)S(1)} %slice.8), channel_id=1, source_target_pairs={{0,16},{8,24},{16,0},{24,8},{1,17},{9,25},{17,1},{25,9},{2,18},{10... | collective-permute-start | bytes 393224 | tf_op jit(solution)/shard_map/ppermute | solution.py:422
  23.2 1.2 %collective-permute-done.6.refs_5_ = f32[2,2,2,32,128]{4,3,2,1,0:T(8,128)S(1)} collective-permute-done((f32[2,2,2,32,128]{4,3,2,1,0:T(8,128)S(1)}, f32[2,2,2,32,128]{4,3,2,1,0:T(8,128)S(1)}, u32[]{:S(2)}, u32[]{:S(2)}) %collective-permute-start.6) | collective-permute-done | bytes 131104 | tf_op jit(solution)/shard_map/ppermute | solution.py:422
  24.5 0.0 collective-permute-start.11
  24.5 2.7 %collective-permute-done.5.refs_4_ = f32[2,2,2,32,128]{4,3,2,1,0:T(8,128)S(1)} collective-permute-done((f32[2,2,2,32,128]{4,3,2,1,0:T(8,128)S(1)}, f32[2,2,2,32,128]{4,3,2,1,0:T(8,128)S(1)}, u32[]{:S(2)}, u32[]{:S(2)}) %collective-permute-start.5) | collective-permute-done | bytes 131104 | tf_op jit(solution)/shard_map/ppermute | solution.py:422
  27.2 0.0 collective-permute-start.10
  27.2 0.0 collective-permute-done.7.refs_6_
  27.2 0.0 collective-permute-done.9.refs_8_
  27.2 0.0 collective-permute-done.8.refs_7_
  27.2 0.0 collective-permute-done.11.refs_10_
  27.2 1.3 %collective-permute-done.10.refs_9_ = f32[2,2,2,32,128]{4,3,2,1,0:T(8,128)S(1)} collective-permute-done((f32[2,2,2,32,128]{4,3,2,1,0:T(8,128)S(1)}, f32[2,2,2,32,128]{4,3,2,1,0:T(8,128)S(1)}, u32[]{:S(2)}, u32[]{:S(2)}) %collective-permute-start.10) | collective-permute-done | bytes 131104 | tf_op jit(solution)/shard_map/ppermute | solution.py:422
  28.5 0.0 copy-done
  28.6 19.5 %shard_map.37 = f32[2,32,128]{2,1,0:T(8,128)} custom-call(s32[2,4]{1,0:T(2,128)S(1)} %copy-done, f32[4,2,2,32,128]{4,3,2,1,0:T(8,128)S(1)} %pad_maximum_fusion.refs_1_, f32[4,2,2,32,128]{4,3,2,1,0:T(8,128)S(1)} %collective-permute-done.3.refs_2_, f32[4,2,2,32,128]{4,3,2,1,0:T(8,128)S(1)} %collective-permute-done.4.refs_3_, ...), custom_call_target="tpu_custom_call" | custom-call | tf_op jit(solution)/shard_map/pallas_call | solution.py:410
  (3 shorter events, 0.0 us)
Async XLA Ops:
  0.8 7.6 %collective-permute-start.2 = (f32[1,2,2,32,128]{4,3,2,1,0:T(8,128)S(1)}, f32[1,2,2,32,128]{4,3,2,1,0:T(8,128)S(1)}, u32[]{:S(2)}, u32[]{:S(2)}) collective-permute-start(f32[1,2,2,32,128]{4,3,2,1,0:T(8,128)S(1)} %maximum_bitcast_fusion), channel_id=1, source_target_pairs={{0,6},{1,7},{2,4},{3,5},{4,2},{5,3},{6,0},{7,1},{8,14},{9,15},{10,... | collective-permute-start | bytes 196616 | tf_op jit(solution)/shard_map/ppermute | solution.py:422
  5.9 5.6 %collective-permute-start.1 = (f32[1,2,2,32,128]{4,3,2,1,0:T(8,128)S(1)}, f32[1,2,2,32,128]{4,3,2,1,0:T(8,128)S(1)}, u32[]{:S(2)}, u32[]{:S(2)}) collective-permute-start(f32[1,2,2,32,128]{4,3,2,1,0:T(8,128)S(1)} %maximum_bitcast_fusion), channel_id=1, source_target_pairs={{0,4},{1,5},{2,6},{3,7},{4,0},{5,1},{6,2},{7,3},{8,12},{9,13},{10,... | collective-permute-start | bytes 196616 | tf_op jit(solution)/shard_map/ppermute | solution.py:422
  5.9 5.6 %collective-permute-start = (f32[1,2,2,32,128]{4,3,2,1,0:T(8,128)S(1)}, f32[1,2,2,32,128]{4,3,2,1,0:T(8,128)S(1)}, u32[]{:S(2)}, u32[]{:S(2)}) collective-permute-start(f32[1,2,2,32,128]{4,3,2,1,0:T(8,128)S(1)} %maximum_bitcast_fusion), channel_id=1, source_target_pairs={{0,2},{1,3},{2,0},{3,1},{4,6},{5,7},{6,4},{7,5},{8,10},{9,11},{10,... | collective-permute-start | bytes 196616 | tf_op jit(solution)/shard_map/ppermute | solution.py:422
  11.5 7.9 %collective-permute-start.4 = (f32[4,2,2,32,128]{4,3,2,1,0:T(8,128)S(1)}, f32[4,2,2,32,128]{4,3,2,1,0:T(8,128)S(1)}, u32[]{:S(2)}, u32[]{:S(2)}) collective-permute-start(f32[4,2,2,32,128]{4,3,2,1,0:T(8,128)S(1)} %pad_maximum_fusion.refs_1_), channel_id=1, source_target_pairs={{0,16},{8,24},{16,0},{24,8},{1,17},{9,25},{17,1},{25,9},{2,18},{10... | collective-permute-start | bytes 786440 | tf_op jit(solution)/shard_map/ppermute | solution.py:422
  13.1 8.1 %collective-permute-start.3 = (f32[4,2,2,32,128]{4,3,2,1,0:T(8,128)S(1)}, f32[4,2,2,32,128]{4,3,2,1,0:T(8,128)S(1)}, u32[]{:S(2)}, u32[]{:S(2)}) collective-permute-start(f32[4,2,2,32,128]{4,3,2,1,0:T(8,128)S(1)} %pad_maximum_fusion.refs_1_), channel_id=1, source_target_pairs={{0,1},{1,0},{2,3},{3,2},{4,5},{5,4},{6,7},{7,6},{8,9},{9,8},{10,11... | collective-permute-start | bytes 786440 | tf_op jit(solution)/shard_map/ppermute | solution.py:422
  14.6 12.6 %collective-permute-start.7 = (f32[4,2,2,32,128]{4,3,2,1,0:T(8,128)S(1)}, f32[4,2,2,32,128]{4,3,2,1,0:T(8,128)S(1)}, u32[]{:S(2)}, u32[]{:S(2)}) collective-permute-start(f32[4,2,2,32,128]{4,3,2,1,0:T(8,128)S(1)} %pad_maximum_fusion.refs_1_), channel_id=1, source_target_pairs={{0,8},{8,0},{16,24},{24,16},{1,9},{9,1},{17,25},{25,17},{2,10},{10... | collective-permute-start | bytes 786440 | tf_op jit(solution)/shard_map/ppermute | solution.py:422
  19.4 9.1 %copy-start = (s32[2,4]{1,0:T(2,128)S(1)}, s32[2,4]{1,0:T(2,128)}, u32[]{:S(2)}) copy-start(s32[2,4]{1,0:T(2,128)} %refs_0_.1) | copy-start | bytes 100
  19.5 5.0 %collective-permute-start.6 = (f32[2,2,2,32,128]{4,3,2,1,0:T(8,128)S(1)}, f32[2,2,2,32,128]{4,3,2,1,0:T(8,128)S(1)}, u32[]{:S(2)}, u32[]{:S(2)}) collective-permute-start(f32[2,2,2,32,128]{4,3,2,1,0:T(8,128)S(1)} %slice.9), channel_id=1, source_target_pairs={{0,1},{1,0},{2,3},{3,2},{4,5},{5,4},{6,7},{7,6},{8,9},{9,8},{10,11... | collective-permute-start | bytes 393224 | tf_op jit(solution)/shard_map/ppermute | solution.py:422
  21.1 6.1 %collective-permute-start.9 = (f32[4,2,2,32,128]{4,3,2,1,0:T(8,128)S(1)}, f32[4,2,2,32,128]{4,3,2,1,0:T(8,128)S(1)}, u32[]{:S(2)}, u32[]{:S(2)}) collective-permute-start(f32[4,2,2,32,128]{4,3,2,1,0:T(8,128)S(1)} %collective-permute-done.4.refs_3_), channel_id=1, source_target_pairs={{0,8},{8,0},{16,24},{24,16},{1,9},{9,1},{17,25},{25,17},{2,10},{10... | collective-permute-start | bytes 786440 | tf_op jit(solution)/shard_map/ppermute | solution.py:422
  21.1 6.1 %collective-permute-start.8 = (f32[4,2,2,32,128]{4,3,2,1,0:T(8,128)S(1)}, f32[4,2,2,32,128]{4,3,2,1,0:T(8,128)S(1)}, u32[]{:S(2)}, u32[]{:S(2)}) collective-permute-start(f32[4,2,2,32,128]{4,3,2,1,0:T(8,128)S(1)} %collective-permute-done.3.refs_2_), channel_id=1, source_target_pairs={{0,8},{8,0},{16,24},{24,16},{1,9},{9,1},{17,25},{25,17},{2,10},{10... | collective-permute-start | bytes 786440 | tf_op jit(solution)/shard_map/ppermute | solution.py:422
  21.7 5.5 %collective-permute-start.5 = (f32[2,2,2,32,128]{4,3,2,1,0:T(8,128)S(1)}, f32[2,2,2,32,128]{4,3,2,1,0:T(8,128)S(1)}, u32[]{:S(2)}, u32[]{:S(2)}) collective-permute-start(f32[2,2,2,32,128]{4,3,2,1,0:T(8,128)S(1)} %slice.8), channel_id=1, source_target_pairs={{0,16},{8,24},{16,0},{24,8},{1,17},{9,25},{17,1},{25,9},{2,18},{10... | collective-permute-start | bytes 393224 | tf_op jit(solution)/shard_map/ppermute | solution.py:422
  24.5 2.7 %collective-permute-start.11 = (f32[2,2,2,32,128]{4,3,2,1,0:T(8,128)S(1)}, f32[2,2,2,32,128]{4,3,2,1,0:T(8,128)S(1)}, u32[]{:S(2)}, u32[]{:S(2)}) collective-permute-start(f32[2,2,2,32,128]{4,3,2,1,0:T(8,128)S(1)} %collective-permute-done.6.refs_5_), channel_id=1, source_target_pairs={{0,8},{8,0},{16,24},{24,16},{1,9},{9,1},{17,25},{25,17},{2,10},{10... | collective-permute-start | bytes 393224 | tf_op jit(solution)/shard_map/ppermute | solution.py:422
  27.2 1.3 %collective-permute-start.10 = (f32[2,2,2,32,128]{4,3,2,1,0:T(8,128)S(1)}, f32[2,2,2,32,128]{4,3,2,1,0:T(8,128)S(1)}, u32[]{:S(2)}, u32[]{:S(2)}) collective-permute-start(f32[2,2,2,32,128]{4,3,2,1,0:T(8,128)S(1)} %collective-permute-done.5.refs_4_), channel_id=1, source_target_pairs={{0,8},{8,0},{16,24},{24,16},{1,9},{9,1},{17,25},{25,17},{2,10},{10... | collective-permute-start | bytes 393224 | tf_op jit(solution)/shard_map/ppermute | solution.py:422
